TPU v7x, 128 devices: a whole 4x4x4 slice. The times are simulated.
128 devices in a mesh: group: 8 (over y_lo, z), dev: 16 (over x, y_hi, core).
Axes of the slice: x: 4, y: 4 (y_hi: 2, y_lo: 2; y = y_hi * 2 + y_lo), z: 4, core: 2. Of those that a mesh axis runs over, the one named last changes fastest.
Arguments:
- field_now: float32 [2, 512, 512, 256], P(None, 'group', 'dev'), may hold values from -6 to 6
- source: float32 [2, 512, 512, 256], P(None, 'group', 'dev'), may hold values from -6 to 6
- wavenumber_sq: float32 [512, 512, 256], P('group', 'dev'), may hold values from 0.02 to 0.2
- shift_sq: float32 [1], replicated, may hold values from 0.05 to 0.2
Outputs:
- field_next: float32 [2, 512, 512, 256], P(None, 'group', 'dev')
All inputs are finite; a program needn't handle non-finite values.
Results may differ from a plain program's by a relative error of at most 0.000092.
Values sent between devices are 32-bit elements; how exact they have to be, the bound alone decides.
A program may use at most 128 MiB of HBM per device.

v0:
```python
import math

import jax
import jax.numpy as jnp
from jax import lax
from jax.sharding import PartitionSpec as P

SWEEPS = 3


RELAX = 0.8
DAMPING = 0.5
HIGHEST = lax.Precision.HIGHEST


def extended(array, sides, width):
    edges = {}
    for axis, dim in sides:
        size, length = (lax.axis_size(axis), array.shape[dim])
        up = [(i, (i + 1) % size) for i in range(size - 1)]
        last = lax.slice_in_dim(array, length - width, length, axis=dim)
        initial = lax.slice_in_dim(array, 0, width, axis=dim)
        edges[dim] = (
            lax.ppermute(last, axis, up),
            lax.ppermute(initial, axis, [(b, a) for a, b in up]),
        )
    done = []
    for _, dim in sides:
        low, high = edges[dim]
        around = [(width, width) if d in done else (0, 0) for d in range(array.ndim)]
        array = jnp.concatenate([jnp.pad(low, around), array, jnp.pad(high, around)], axis=dim)
        done.append(dim)
    return array


def operate(padded, wave_sq):
    centre = padded[:, 1:-1, 1:-1, :]
    beside = padded[:, 2:, 1:-1, :] + padded[:, :-2, 1:-1, :]
    beside = beside + padded[:, 1:-1, 2:, :] + padded[:, 1:-1, :-2, :]
    vertical = jnp.pad(centre, ((0, 0), (0, 0), (0, 0), (1, 1)))
    beside = beside + vertical[..., 2:] + vertical[..., :-2]
    layers = centre.shape[-1]
    height = lax.broadcasted_iota(jnp.int32, (1, 1, layers), 2)
    boundary = jnp.logical_or(height == 0, height == layers - 1).astype(wave_sq.dtype)
    absorb = jnp.sqrt(wave_sq)
    robin = jnp.stack([centre[0] - absorb * centre[1], centre[1] + absorb * centre[0]]) * boundary
    return (6.0 - wave_sq) * centre - beside - robin


def fourier_table(count, sign, real_type):
    index_row = lax.broadcasted_iota(jnp.int32, (count, count), 0)
    index_col = lax.broadcasted_iota(jnp.int32, (count, count), 1)
    angle = 2.0 * math.pi / count * (index_row * index_col % count).astype(real_type)
    cosine = jnp.cos(angle)
    sine = sign * jnp.sin(angle)
    scale = 1.0 if sign < 0 else 1.0 / count
    return scale * jnp.stack([jnp.stack([cosine, sine]), jnp.stack([-sine, cosine])])


def vertical_basis(layers, real_type):
    index_row = lax.broadcasted_iota(jnp.int32, (layers, layers), 0) + 1
    index_col = lax.broadcasted_iota(jnp.int32, (layers, layers), 1) + 1
    angle = math.pi / (layers + 1) * (index_row * index_col % (2 * (layers + 1))).astype(real_type)
    return math.sqrt(2.0 / (layers + 1)) * jnp.sin(angle)


def horizontal_eigen(wave_index, count, real_type):
    angle = 2.0 * math.pi / count * wave_index.astype(real_type)
    return (2.0 - 2.0 * jnp.cos(angle)) / 16.0


def vertical_eigen(mode_index, layers, real_type):
    angle = math.pi / (layers + 1) * (mode_index + 1).astype(real_type)
    return 2.0 - 2.0 * jnp.cos(angle)


def divide_modes(modes, eigen, shift):
    real_part = eigen - shift
    imag_part = -DAMPING * shift
    modulus = real_part * real_part + imag_part * imag_part
    upper = (modes[0] * real_part + modes[1] * imag_part) / modulus
    lower = (modes[1] * real_part - modes[0] * imag_part) / modulus
    return jnp.stack([upper, lower])


def restrict(residual):
    extent = residual.shape
    blocks = residual.reshape(2, extent[1] // 4, 4, extent[2] // 4, 4, extent[3])
    return jnp.mean(blocks, axis=(2, 4))


def prolong(coarse):
    extent = coarse.shape
    spread = jnp.broadcast_to(
        coarse[:, :, None, :, None, :], (2, extent[1], 4, extent[2], 4, extent[3])
    )
    return spread.reshape(2, extent[1] * 4, extent[2] * 4, extent[3])


def body(field_now, source, wavenumber_sq, shift_sq):
    real_type = field_now.dtype
    padded = extended(field_now, (("group", 1), ("dev", 2)), 1)
    residual = source - operate(padded, wavenumber_sq)
    coarse = restrict(residual)
    groups = lax.axis_size("group")
    members = lax.axis_size("dev")
    cells_x = coarse.shape[1]
    cells_y = coarse.shape[2]
    layers = coarse.shape[3]
    waves_x = cells_x * groups
    waves_y = cells_y * members
    shift = shift_sq[0]
    basis = vertical_basis(layers, real_type)
    modes = jnp.einsum("cxyz,zm->cmxy", coarse, basis, precision=HIGHEST)
    flat = modes.reshape(2, layers, 1, cells_x * cells_y)
    gathered = lax.all_to_all(flat, ("group", "dev"), split_axis=1, concat_axis=2, tiled=True)
    local_modes = gathered.shape[1]
    planes = gathered.reshape(2, local_modes, groups, members, cells_x, cells_y)
    planes = planes.transpose(0, 1, 2, 4, 3, 5).reshape(2, local_modes, waves_x, waves_y)
    planes = jnp.einsum(
        "cmxy,cdyk->dmxk", planes, fourier_table(waves_y, -1, real_type), precision=HIGHEST
    )
    planes = jnp.einsum(
        "cmxk,cdxj->dmjk", planes, fourier_table(waves_x, -1, real_type), precision=HIGHEST
    )
    first_mode = (lax.axis_index("group") * members + lax.axis_index("dev")) * local_modes
    mode_index = first_mode + lax.broadcasted_iota(jnp.int32, (local_modes, 1, 1), 0)
    wave_x = lax.broadcasted_iota(jnp.int32, (1, waves_x, 1), 1)
    wave_y = lax.broadcasted_iota(jnp.int32, (1, 1, waves_y), 2)
    eigen = (
        vertical_eigen(mode_index, layers, real_type)
        + horizontal_eigen(wave_x, waves_x, real_type)
        + horizontal_eigen(wave_y, waves_y, real_type)
    )
    planes = divide_modes(planes, eigen, shift)
    planes = jnp.einsum(
        "cmjk,cdjx->dmxk", planes, fourier_table(waves_x, 1, real_type), precision=HIGHEST
    )
    planes = jnp.einsum(
        "cmxk,cdky->dmxy", planes, fourier_table(waves_y, 1, real_type), precision=HIGHEST
    )
    planes = planes.reshape(2, local_modes, groups, cells_x, members, cells_y).transpose(
        0, 1, 2, 4, 3, 5
    )
    planes = planes.reshape(2, local_modes, groups * members, cells_x * cells_y)
    modes = lax.all_to_all(
        planes, ("group", "dev"), split_axis=2, concat_axis=1, tiled=True
    ).reshape(2, layers, cells_x, cells_y)
    correction = jnp.einsum("cmxy,mz->cxyz", modes, basis, precision=HIGHEST)
    field = field_now + prolong(correction)
    weight = RELAX / (6.0 - wavenumber_sq)
    for sweep_index in range(SWEEPS):
        padded = extended(field, (("group", 1), ("dev", 2)), 1)
        field = field + weight * (source - operate(padded, wavenumber_sq))
    return field


def solution(mesh):
    return jax.shard_map(
        body,
        mesh=mesh,
        in_specs=(
            P(None, "group", "dev", None),
            P(None, "group", "dev", None),
            P("group", "dev", None),
            P(),
        ),
        out_specs=P(None, "group", "dev", None),
        check_vma=False,
    )
```

profile of v0, /device:TPU:25, one launch (start us, length us, event | category | flops | bytes accessed | tf_op | source)
XLA Modules:
  0.0 250.1 jit_solution(13960402044666753848)
XLA Ops:
  0.0 1.5 fusion.112
  1.5 5.8 %collective-permute-start = (f32[2,1,32,256]{3,2,1,0:T(8,128)}, f32[2,1,32,256]{3,2,1,0:T(8,128)S(1)}, u32[]{:S(2)}, u32[]{:S(2)}) collective-permute-start(f32[2,1,32,256]{3,2,1,0:T(8,128)} %get-tuple-element.27), channel_id=1, source_target_pairs={{16,0},{32,16},{48,32},{64,48},{80,64},{96,80},{112,96},{17,1},{33... | collective-permute-start | bytes 196616 | tf_op jit(solution)/shard_map/ppermute | solution.py:25
  7.4 1.9 collective-permute-start.1
  9.3 2.4 fusion.111
  11.7 2.9 %collective-permute-start.2 = (f32[2,64,1,256]{3,2,1,0:T(1,128)}, f32[2,64,1,256]{3,2,1,0:T(1,128)}, u32[]{:S(2)}, u32[]{:S(2)}) collective-permute-start(f32[2,64,1,256]{3,2,1,0:T(1,128)} %get-tuple-element.25), channel_id=1, source_target_pairs={{1,0},{2,1},{3,2},{4,3},{5,4},{6,5},{7,6},{8,7},{9,8},{10,9},{11,1... | collective-permute-start | bytes 393224 | tf_op jit(solution)/shard_map/ppermute | solution.py:25
  14.6 5.1 %collective-permute-start.3 = (f32[2,64,1,256]{3,2,1,0:T(1,128)}, f32[2,64,1,256]{3,2,1,0:T(1,128)}, u32[]{:S(2)}, u32[]{:S(2)}) collective-permute-start(f32[2,64,1,256]{3,2,1,0:T(1,128)} %get-tuple-element.26), channel_id=1, source_target_pairs={{0,1},{1,2},{2,3},{3,4},{4,5},{5,6},{6,7},{7,8},{8,9},{9,10},{10,1... | collective-permute-start | bytes 393224 | tf_op jit(solution)/shard_map/ppermute | solution.py:24
  20.5 7.2 %fusion.47 = (f32[1,64,32,256]{3,2,1,0:T(8,128)}, f32[1,64,32,256]{3,2,1,0:T(8,128)}, f32[64,32,256]{2,1,0:T(8,128)}) fusion(f32[2,64,32,256]{3,2,1,0:T(8,128)} %param.4, f32[64,32,256]{2,1,0:T(8,128)} %param.6), kind=kLoop, calls=%fused_computation.99 | loop fusion | flops 2621440 | bytes 12582912 | tf_op jit(solution)/shard_map/stack | solution.py:46
  27.8 0.6 constant_dynamic-update-slice_fusion.2
  28.5 4.9 %constant_dynamic-update-slice_fusion.1 = f32[2,66,32,256]{3,2,1,0:T(8,128)} fusion(f32[2,66,32,256]{3,2,1,0:T(8,128)} %constant_dynamic-update-slice_fusion.2, f32[2,64,32,256]{3,2,1,0:T(8,128)} %param.4), kind=kLoop, calls=%fused_computation.177 | loop fusion | bytes 8388608
  34.0 10.6 %fusion.4 = f32[2,64,32,256]{3,2,1,0:T(8,128)} fusion(f32[2,64,32,256]{3,2,1,0:T(8,128)} %param.5, f32[2,64,32,256]{3,2,1,0:T(8,128)S(1)} %copy-done, f32[2,66,32,256]{3,2,1,0:T(8,128)} %constant_dynamic-update-slice_fusion, f32[2,64,1,256]{3,2,1,0:T(1,128)} %collective-permute-done.3, f32[2,64,1,256]{3,2,1,0:T(1,128)} %collective-permute-done.2, ...), kind=kLoop, calls=%fused_computation.12 | loop fusion | flops 22020096 | bytes 23593984 | tf_op jit(solution)/shard_map/sub | solution.py:103
  44.7 5.2 %reshape.207 = f32[2,16,4,8,4,256]{5,4,3,2,1,0:T(4,128)} reshape(f32[2,64,32,256]{3,2,1,0:T(8,128)} %fusion.4) | data formatting | bytes 8388608 | tf_op jit(solution)/shard_map/reshape | solution.py:88
  49.8 3.5 %reduce_sum.9 = f32[2,16,8,256]{3,2,1,0:T(8,128)S(1)} reduce(f32[2,16,4,8,4,256]{5,4,3,2,1,0:T(4,128)} %reshape.207, f32[]{:T(128)} %constant.78.clone.1), dimensions={2,4}, to_apply=%region_0.1 | reduce | flops 983040 | bytes 4456452 | tf_op jit(solution)/shard_map/reduce_sum | solution.py:89
  53.4 1.5 convolution_bitcast_fusion.4
  55.1 0.8 copy.31
  55.9 9.6 %all-to-all-start = ((f32[2,256,1,128]{3,0,2,1:T(2,128)}), f32[2,256,1,128]{3,0,2,1:T(2,128)S(1)}, u32[]{:S(2)}, u32[]{:S(2)}) async-start(f32[2,256,1,128]{3,0,2,1:T(2,128)} %copy.31), calls=%async_computation | async-start | bytes 524288 | tf_op jit(solution)/shard_map/all_to_all | solution.py:116
  66.3 8.7 %all-to-all-done = f32[2,256,1,128]{3,0,2,1:T(2,128)S(1)} async-done(((f32[2,256,1,128]{3,0,2,1:T(2,128)}), f32[2,256,1,128]{3,0,2,1:T(2,128)S(1)}, u32[]{:S(2)}, u32[]{:S(2)}) %all-to-all-start) | async-done | bytes 262176 | tf_op jit(solution)/shard_map/all_to_all | solution.py:116
  75.8 2.9 %copy.34 = f32[2,2,8,16,16,8]{3,2,5,4,1,0:T(8,128)} copy(f32[2,2,8,16,16,8]{4,2,5,3,1,0:T(8,128)S(1)} %bitcast.166) | data formatting | bytes 524288 | tf_op jit(solution)/shard_map/transpose | solution.py:119
  78.7 2.2 reshape.210
  83.2 2.9 %copy.40 = f32[2,2,8,16,16,8]{4,2,5,3,1,0:T(8,128)} copy(f32[2,2,8,16,16,8]{3,2,5,4,1,0:T(8,128)S(1)} %reshape.211) | data formatting | bytes 524288 | tf_op jit(solution)/shard_map/reshape | solution.py:142
  86.1 2.2 reshape.212
  88.5 14.8 %all_to_all.30 = f32[2,2,128,128]{3,1,0,2:T(2,128)S(1)} all-to-all(f32[2,2,128,128]{3,1,0,2:T(2,128)S(1)} %copy.41), channel_id=1, replica_groups=mesh['group'=8,'dev'=16] {'group','dev'}, dimensions={2} | all-to-all | bytes 524288 | tf_op jit(solution)/shard_map/all_to_all | solution.py:146
  103.3 3.7 %reshape.213 = f32[2,256,16,8]{3,2,1,0:T(8,128)} reshape(f32[2,128,2,1,128]{4,2,1,0,3:T(2,128)S(1)} %copy.42) | data formatting | bytes 524288 | tf_op jit(solution)/shard_map/reshape | solution.py:148
  107.0 10.1 %fusion.44 = f32[2,16,8,256]{3,2,1,0:T(8,128)S(1)} fusion(f32[2,256,16,8]{3,2,1,0:T(8,128)} %reshape.213, s32[256]{0:T(256)S(1)} %iota_add_fusion), kind=kOutput, calls=%fused_computation.88 | convolution fusion | flops 201981952 | bytes 525312 | tf_op jit(solution)/shard_map/cmxy,mz->cxyz/dot_general | solution.py:149
  117.1 3.1 %broadcast_in_dim.2 = f32[2,16,4,8,4,256]{5,4,3,2,1,0:T(4,128)} broadcast(f32[2,16,8,256]{3,2,1,0:T(8,128)S(1)} %fusion.44), dimensions={0,1,3,5} | broadcast | bytes 4456448 | tf_op jit(solution)/shard_map/broadcast_in_dim | solution.py:94
  120.2 5.3 %reshape.214 = f32[2,64,32,256]{3,2,1,0:T(8,128)} reshape(f32[2,16,4,8,4,256]{5,4,3,2,1,0:T(4,128)} %broadcast_in_dim.2) | data formatting | bytes 8388608 | tf_op jit(solution)/shard_map/reshape | solution.py:97
  125.5 4.6 %add.277 = f32[2,64,32,256]{3,2,1,0:T(8,128)S(1)} add(f32[2,64,32,256]{3,2,1,0:T(8,128)} %param.4, f32[2,64,32,256]{3,2,1,0:T(8,128)} %reshape.214) | non-fusion elementwise | flops 1048576 | bytes 12582912 | tf_op jit(solution)/shard_map/add | solution.py:150
  130.3 2.5 collective-permute-start.5
  132.7 4.9 %collective-permute-start.4 = (f32[2,1,32,256]{3,2,1,0:T(8,128)S(1)}, f32[2,1,32,256]{3,2,1,0:T(8,128)S(1)}, u32[]{:S(2)}, u32[]{:S(2)}) collective-permute-start(f32[2,1,32,256]{3,2,1,0:T(8,128)S(1)} %get-tuple-element.24), channel_id=1, source_target_pairs={{16,0},{32,16},{48,32},{64,48},{80,64},{96,80},{112,96},{17,1},{33... | collective-permute-start | bytes 196616 | tf_op jit(solution)/shard_map/ppermute | solution.py:25
  137.7 2.9 %collective-permute-start.6 = (f32[2,64,1,256]{3,2,1,0:T(1,128)S(1)}, f32[2,64,1,256]{3,2,1,0:T(1,128)S(1)}, u32[]{:S(2)}, u32[]{:S(2)}) collective-permute-start(f32[2,64,1,256]{3,2,1,0:T(1,128)S(1)} %get-tuple-element.21), channel_id=1, source_target_pairs={{1,0},{2,1},{3,2},{4,3},{5,4},{6,5},{7,6},{8,7},{9,8},{10,9},{11,1... | collective-permute-start | bytes 393224 | tf_op jit(solution)/shard_map/ppermute | solution.py:25
  140.6 5.5 %collective-permute-start.7 = (f32[2,64,1,256]{3,2,1,0:T(1,128)S(1)}, f32[2,64,1,256]{3,2,1,0:T(1,128)S(1)}, u32[]{:S(2)}, u32[]{:S(2)}) collective-permute-start(f32[2,64,1,256]{3,2,1,0:T(1,128)S(1)} %get-tuple-element.22), channel_id=1, source_target_pairs={{0,1},{1,2},{2,3},{3,4},{4,5},{5,6},{6,7},{7,8},{8,9},{9,10},{10,1... | collective-permute-start | bytes 393224 | tf_op jit(solution)/shard_map/ppermute | solution.py:24
  146.1 3.8 %subtract_bitcast_fusion.2 = (f32[1,64,32,256]{3,2,1,0:T(8,128)}, f32[1,64,32,256]{3,2,1,0:T(8,128)}, f32[64,32,256]{2,1,0:T(8,128)}) fusion(f32[2,64,32,256]{3,2,1,0:T(8,128)S(1)} %add.277, f32[64,32,256]{2,1,0:T(8,128)S(1)} %copy-done.3), kind=kLoop, calls=%fused_computation.107 | loop fusion | flops 3145728 | bytes 12582912 | tf_op jit(solution)/shard_map/stack | solution.py:46
  149.9 17.5 %fusion.11 = f32[2,64,32,256]{3,2,1,0:T(8,128)} fusion(f32[2,64,32,256]{3,2,1,0:T(8,128)} %copy-done.2, f32[2,64,32,256]{3,2,1,0:T(8,128)} %param.5, f32[2,64,1,256]{3,2,1,0:T(1,128)S(1)} %collective-permute-done.7, f32[2,1,32,256]{3,2,1,0:T(8,128)S(1)} %collective-permute-done.4, f32[2,1,32,256]{3,2,1,0:T(8,128)S(1)} %collective-permute-done.5, ...), kind=kLoop, calls=%fused_computation.19 | loop fusion | flops 28311552 | bytes 21365760 | tf_op jit(solution)/shard_map/add | solution.py:154
  167.4 0.9 fusion.108
  168.3 1.7 fusion.107
  170.0 1.9 collective-permute-start.9
  171.9 5.5 %collective-permute-start.8 = (f32[2,1,32,256]{3,2,1,0:T(8,128)S(1)}, f32[2,1,32,256]{3,2,1,0:T(8,128)S(1)}, u32[]{:S(2)}, u32[]{:S(2)}) collective-permute-start(f32[2,1,32,256]{3,2,1,0:T(8,128)S(1)} %get-tuple-element.20), channel_id=1, source_target_pairs={{16,0},{32,16},{48,32},{64,48},{80,64},{96,80},{112,96},{17,1},{33... | collective-permute-start | bytes 196616 | tf_op jit(solution)/shard_map/ppermute | solution.py:25
  177.4 2.2 collective-permute-start.10
  179.6 5.8 %collective-permute-start.11 = (f32[2,64,1,256]{3,2,1,0:T(1,128)S(1)}, f32[2,64,1,256]{3,2,1,0:T(1,128)S(1)}, u32[]{:S(2)}, u32[]{:S(2)}) collective-permute-start(f32[2,64,1,256]{3,2,1,0:T(1,128)S(1)} %get-tuple-element.18), channel_id=1, source_target_pairs={{0,1},{1,2},{2,3},{3,4},{4,5},{5,6},{6,7},{7,8},{8,9},{9,10},{10,1... | collective-permute-start | bytes 393224 | tf_op jit(solution)/shard_map/ppermute | solution.py:24
  185.4 6.2 %subtract_bitcast_fusion.1 = (f32[1,64,32,256]{3,2,1,0:T(8,128)}, f32[1,64,32,256]{3,2,1,0:T(8,128)}) fusion(f32[2,64,32,256]{3,2,1,0:T(8,128)} %fusion.11, f32[64,32,256]{2,1,0:T(8,128)} %param.6), kind=kLoop, calls=%fused_computation.105 | loop fusion | flops 2097152 | bytes 10485760 | tf_op jit(solution)/shard_map/stack | solution.py:46
  191.6 17.4 %fusion.18 = f32[2,64,32,256]{3,2,1,0:T(8,128)} fusion(f32[2,64,32,256]{3,2,1,0:T(8,128)} %fusion.11, f32[2,64,32,256]{3,2,1,0:T(8,128)} %param.5, f32[2,64,1,256]{3,2,1,0:T(1,128)S(1)} %collective-permute-done.11, f32[2,1,32,256]{3,2,1,0:T(8,128)S(1)} %collective-permute-done.8, f32[2,1,32,256]{3,2,1,0:T(8,128)S(1)} %collective-permute-done.9, ...), kind=kLoop, calls=%fused_computation.26 | loop fusion | flops 28311552 | bytes 21365760 | tf_op jit(solution)/shard_map/add | solution.py:154
  209.0 0.9 fusion.106
  209.9 1.7 fusion.105
  211.6 1.9 collective-permute-start.13
  213.5 5.5 %collective-permute-start.12 = (f32[2,1,32,256]{3,2,1,0:T(8,128)S(1)}, f32[2,1,32,256]{3,2,1,0:T(8,128)S(1)}, u32[]{:S(2)}, u32[]{:S(2)}) collective-permute-start(f32[2,1,32,256]{3,2,1,0:T(8,128)S(1)} %get-tuple-element.16), channel_id=1, source_target_pairs={{16,0},{32,16},{48,32},{64,48},{80,64},{96,80},{112,96},{17,1},{33... | collective-permute-start | bytes 196616 | tf_op jit(solution)/shard_map/ppermute | solution.py:25
  219.0 1.9 collective-permute-start.14
  221.0 6.0 %collective-permute-start.15 = (f32[2,64,1,256]{3,2,1,0:T(1,128)S(1)}, f32[2,64,1,256]{3,2,1,0:T(1,128)S(1)}, u32[]{:S(2)}, u32[]{:S(2)}) collective-permute-start(f32[2,64,1,256]{3,2,1,0:T(1,128)S(1)} %get-tuple-element.14), channel_id=1, source_target_pairs={{0,1},{1,2},{2,3},{3,4},{4,5},{5,6},{6,7},{7,8},{8,9},{9,10},{10,1... | collective-permute-start | bytes 393224 | tf_op jit(solution)/shard_map/ppermute | solution.py:24
  227.0 6.1 %subtract_bitcast_fusion = (f32[1,64,32,256]{3,2,1,0:T(8,128)}, f32[1,64,32,256]{3,2,1,0:T(8,128)}) fusion(f32[2,64,32,256]{3,2,1,0:T(8,128)} %fusion.18, f32[64,32,256]{2,1,0:T(8,128)} %param.6), kind=kLoop, calls=%fused_computation.103 | loop fusion | flops 2097152 | bytes 10485760 | tf_op jit(solution)/shard_map/stack | solution.py:46
  233.2 16.9 %fusion.25 = f32[2,64,32,256]{3,2,1,0:T(8,128)} fusion(f32[2,64,32,256]{3,2,1,0:T(8,128)} %fusion.18, f32[2,64,32,256]{3,2,1,0:T(8,128)} %param.5, f32[2,64,1,256]{3,2,1,0:T(1,128)S(1)} %collective-permute-done.15, f32[2,1,32,256]{3,2,1,0:T(8,128)S(1)} %collective-permute-done.12, f32[2,1,32,256]{3,2,1,0:T(8,128)S(1)} %collective-permute-done.13, ...), kind=kLoop, calls=%fused_computation.33 | loop fusion | flops 28311552 | bytes 21365760 | tf_op jit(solution)/shard_map/add | solution.py:154
  (50 shorter events, 5.4 us)
Async XLA Ops:
  1.5 31.9 %collective-permute-start = (f32[2,1,32,256]{3,2,1,0:T(8,128)}, f32[2,1,32,256]{3,2,1,0:T(8,128)S(1)}, u32[]{:S(2)}, u32[]{:S(2)}) collective-permute-start(f32[2,1,32,256]{3,2,1,0:T(8,128)} %get-tuple-element.27), channel_id=1, source_target_pairs={{16,0},{32,16},{48,32},{64,48},{80,64},{96,80},{112,96},{17,1},{33... | collective-permute-start | bytes 196616 | tf_op jit(solution)/shard_map/ppermute | solution.py:25
  7.4 20.5 %collective-permute-start.1 = (f32[2,1,32,256]{3,2,1,0:T(8,128)S(1)}, f32[2,1,32,256]{3,2,1,0:T(8,128)S(1)}, u32[]{:S(2)}, u32[]{:S(2)}) collective-permute-start(f32[2,1,32,256]{3,2,1,0:T(8,128)S(1)} %get-tuple-element.28), channel_id=1, source_target_pairs={{0,16},{16,32},{32,48},{48,64},{64,80},{80,96},{96,112},{1,17},{17... | collective-permute-start | bytes 196616 | tf_op jit(solution)/shard_map/ppermute | solution.py:24
  11.7 22.3 %collective-permute-start.2 = (f32[2,64,1,256]{3,2,1,0:T(1,128)}, f32[2,64,1,256]{3,2,1,0:T(1,128)}, u32[]{:S(2)}, u32[]{:S(2)}) collective-permute-start(f32[2,64,1,256]{3,2,1,0:T(1,128)} %get-tuple-element.25), channel_id=1, source_target_pairs={{1,0},{2,1},{3,2},{4,3},{5,4},{6,5},{7,6},{8,7},{9,8},{10,9},{11,1... | collective-permute-start | bytes 393224 | tf_op jit(solution)/shard_map/ppermute | solution.py:25
  14.6 19.5 %collective-permute-start.3 = (f32[2,64,1,256]{3,2,1,0:T(1,128)}, f32[2,64,1,256]{3,2,1,0:T(1,128)}, u32[]{:S(2)}, u32[]{:S(2)}) collective-permute-start(f32[2,64,1,256]{3,2,1,0:T(1,128)} %get-tuple-element.26), channel_id=1, source_target_pairs={{0,1},{1,2},{2,3},{3,4},{4,5},{5,6},{6,7},{7,8},{8,9},{9,10},{10,1... | collective-permute-start | bytes 393224 | tf_op jit(solution)/shard_map/ppermute | solution.py:24
  28.5 5.6 %copy-start = (f32[2,64,32,256]{3,2,1,0:T(8,128)S(1)}, f32[2,64,32,256]{3,2,1,0:T(8,128)}, u32[]{:S(2)}) copy-start(f32[2,64,32,256]{3,2,1,0:T(8,128)} %param.4) | copy-start | bytes 12582916
  55.9 19.1 %all-to-all-start = ((f32[2,256,1,128]{3,0,2,1:T(2,128)}), f32[2,256,1,128]{3,0,2,1:T(2,128)S(1)}, u32[]{:S(2)}, u32[]{:S(2)}) async-start(f32[2,256,1,128]{3,0,2,1:T(2,128)} %copy.31), calls=%async_computation | async-start | bytes 524288 | tf_op jit(solution)/shard_map/all_to_all | solution.py:116
  125.5 20.6 %copy-start.3 = (f32[64,32,256]{2,1,0:T(8,128)S(1)}, f32[64,32,256]{2,1,0:T(8,128)}, u32[]{:S(2)}) copy-start(f32[64,32,256]{2,1,0:T(8,128)} %param.6) | copy-start | bytes 6291460
  130.1 19.8 %copy-start.2 = (f32[2,64,32,256]{3,2,1,0:T(8,128)}, f32[2,64,32,256]{3,2,1,0:T(8,128)S(1)}, u32[]{:S(2)}) copy-start(f32[2,64,32,256]{3,2,1,0:T(8,128)S(1)} %add.277) | copy-start | bytes 12582916
  130.3 19.6 %collective-permute-start.5 = (f32[2,1,32,256]{3,2,1,0:T(8,128)S(1)}, f32[2,1,32,256]{3,2,1,0:T(8,128)S(1)}, u32[]{:S(2)}, u32[]{:S(2)}) collective-permute-start(f32[2,1,32,256]{3,2,1,0:T(8,128)S(1)} %get-tuple-element.23), channel_id=1, source_target_pairs={{0,16},{16,32},{32,48},{48,64},{64,80},{80,96},{96,112},{1,17},{17... | collective-permute-start | bytes 196616 | tf_op jit(solution)/shard_map/ppermute | solution.py:24
  132.7 17.1 %collective-permute-start.4 = (f32[2,1,32,256]{3,2,1,0:T(8,128)S(1)}, f32[2,1,32,256]{3,2,1,0:T(8,128)S(1)}, u32[]{:S(2)}, u32[]{:S(2)}) collective-permute-start(f32[2,1,32,256]{3,2,1,0:T(8,128)S(1)} %get-tuple-element.24), channel_id=1, source_target_pairs={{16,0},{32,16},{48,32},{64,48},{80,64},{96,80},{112,96},{17,1},{33... | collective-permute-start | bytes 196616 | tf_op jit(solution)/shard_map/ppermute | solution.py:25
  137.7 12.2 %collective-permute-start.6 = (f32[2,64,1,256]{3,2,1,0:T(1,128)S(1)}, f32[2,64,1,256]{3,2,1,0:T(1,128)S(1)}, u32[]{:S(2)}, u32[]{:S(2)}) collective-permute-start(f32[2,64,1,256]{3,2,1,0:T(1,128)S(1)} %get-tuple-element.21), channel_id=1, source_target_pairs={{1,0},{2,1},{3,2},{4,3},{5,4},{6,5},{7,6},{8,7},{9,8},{10,9},{11,1... | collective-permute-start | bytes 393224 | tf_op jit(solution)/shard_map/ppermute | solution.py:25
  140.6 9.3 %copy-start.1 = (f32[64,32,256]{2,1,0:T(8,128)S(1)}, f32[64,32,256]{2,1,0:T(8,128)}, u32[]{:S(2)}) copy-start(f32[64,32,256]{2,1,0:T(8,128)} %get-tuple-element.30) | copy-start | bytes 6291460
  140.6 9.3 %collective-permute-start.7 = (f32[2,64,1,256]{3,2,1,0:T(1,128)S(1)}, f32[2,64,1,256]{3,2,1,0:T(1,128)S(1)}, u32[]{:S(2)}, u32[]{:S(2)}) collective-permute-start(f32[2,64,1,256]{3,2,1,0:T(1,128)S(1)} %get-tuple-element.22), channel_id=1, source_target_pairs={{0,1},{1,2},{2,3},{3,4},{4,5},{5,6},{6,7},{7,8},{8,9},{9,10},{10,1... | collective-permute-start | bytes 393224 | tf_op jit(solution)/shard_map/ppermute | solution.py:24
  170.0 21.6 %collective-permute-start.9 = (f32[2,1,32,256]{3,2,1,0:T(8,128)S(1)}, f32[2,1,32,256]{3,2,1,0:T(8,128)S(1)}, u32[]{:S(2)}, u32[]{:S(2)}) collective-permute-start(f32[2,1,32,256]{3,2,1,0:T(8,128)S(1)} %get-tuple-element.19), channel_id=1, source_target_pairs={{0,16},{16,32},{32,48},{48,64},{64,80},{80,96},{96,112},{1,17},{17... | collective-permute-start | bytes 196616 | tf_op jit(solution)/shard_map/ppermute | solution.py:24
  171.9 19.6 %collective-permute-start.8 = (f32[2,1,32,256]{3,2,1,0:T(8,128)S(1)}, f32[2,1,32,256]{3,2,1,0:T(8,128)S(1)}, u32[]{:S(2)}, u32[]{:S(2)}) collective-permute-start(f32[2,1,32,256]{3,2,1,0:T(8,128)S(1)} %get-tuple-element.20), channel_id=1, source_target_pairs={{16,0},{32,16},{48,32},{64,48},{80,64},{96,80},{112,96},{17,1},{33... | collective-permute-start | bytes 196616 | tf_op jit(solution)/shard_map/ppermute | solution.py:25
  177.4 14.2 %collective-permute-start.10 = (f32[2,64,1,256]{3,2,1,0:T(1,128)S(1)}, f32[2,64,1,256]{3,2,1,0:T(1,128)S(1)}, u32[]{:S(2)}, u32[]{:S(2)}) collective-permute-start(f32[2,64,1,256]{3,2,1,0:T(1,128)S(1)} %get-tuple-element.17), channel_id=1, source_target_pairs={{1,0},{2,1},{3,2},{4,3},{5,4},{6,5},{7,6},{8,7},{9,8},{10,9},{11,1... | collective-permute-start | bytes 393224 | tf_op jit(solution)/shard_map/ppermute | solution.py:25
  179.6 12.0 %collective-permute-start.11 = (f32[2,64,1,256]{3,2,1,0:T(1,128)S(1)}, f32[2,64,1,256]{3,2,1,0:T(1,128)S(1)}, u32[]{:S(2)}, u32[]{:S(2)}) collective-permute-start(f32[2,64,1,256]{3,2,1,0:T(1,128)S(1)} %get-tuple-element.18), channel_id=1, source_target_pairs={{0,1},{1,2},{2,3},{3,4},{4,5},{5,6},{6,7},{7,8},{8,9},{9,10},{10,1... | collective-permute-start | bytes 393224 | tf_op jit(solution)/shard_map/ppermute | solution.py:24
  211.6 21.5 %collective-permute-start.13 = (f32[2,1,32,256]{3,2,1,0:T(8,128)S(1)}, f32[2,1,32,256]{3,2,1,0:T(8,128)S(1)}, u32[]{:S(2)}, u32[]{:S(2)}) collective-permute-start(f32[2,1,32,256]{3,2,1,0:T(8,128)S(1)} %get-tuple-element.15), channel_id=1, source_target_pairs={{0,16},{16,32},{32,48},{48,64},{64,80},{80,96},{96,112},{1,17},{17... | collective-permute-start | bytes 196616 | tf_op jit(solution)/shard_map/ppermute | solution.py:24
  213.5 19.6 %collective-permute-start.12 = (f32[2,1,32,256]{3,2,1,0:T(8,128)S(1)}, f32[2,1,32,256]{3,2,1,0:T(8,128)S(1)}, u32[]{:S(2)}, u32[]{:S(2)}) collective-permute-start(f32[2,1,32,256]{3,2,1,0:T(8,128)S(1)} %get-tuple-element.16), channel_id=1, source_target_pairs={{16,0},{32,16},{48,32},{64,48},{80,64},{96,80},{112,96},{17,1},{33... | collective-permute-start | bytes 196616 | tf_op jit(solution)/shard_map/ppermute | solution.py:25
  219.0 14.1 %collective-permute-start.14 = (f32[2,64,1,256]{3,2,1,0:T(1,128)S(1)}, f32[2,64,1,256]{3,2,1,0:T(1,128)S(1)}, u32[]{:S(2)}, u32[]{:S(2)}) collective-permute-start(f32[2,64,1,256]{3,2,1,0:T(1,128)S(1)} %get-tuple-element.13), channel_id=1, source_target_pairs={{1,0},{2,1},{3,2},{4,3},{5,4},{6,5},{7,6},{8,7},{9,8},{10,9},{11,1... | collective-permute-start | bytes 393224 | tf_op jit(solution)/shard_map/ppermute | solution.py:25
  221.0 12.2 %collective-permute-start.15 = (f32[2,64,1,256]{3,2,1,0:T(1,128)S(1)}, f32[2,64,1,256]{3,2,1,0:T(1,128)S(1)}, u32[]{:S(2)}, u32[]{:S(2)}) collective-permute-start(f32[2,64,1,256]{3,2,1,0:T(1,128)S(1)} %get-tuple-element.14), channel_id=1, source_target_pairs={{0,1},{1,2},{2,3},{3,4},{4,5},{5,6},{6,7},{7,8},{8,9},{9,10},{10,1... | collective-permute-start | bytes 393224 | tf_op jit(solution)/shard_map/ppermute | solution.py:24
where the time goes:
time: 251 us; the launch traced here: 250 us
  other arithmetic  95 us (38%)
  starting transfers between devices  71.8 us (29%)
  local copies, waits for them, and re-layouts  45.5 us (18%)
  blocking collectives  14.8 us (6%)
  matrix products  13.1 us (5%)
  waiting for transfers between devices  8.74 us (3%)
    add x3, other arithmetic, body(): field = field + weight * (source - operate(padded, wavenumber_sq))  51.8 us
    ppermute x8, starting transfers between devices, extended(): lax.ppermute(initial, axis, [(b, a) for a, b in up])  31.5 us
    ppermute x8, starting transfers between devices, extended(): lax.ppermute(last, axis, up)  30.7 us
    another operation x4, other arithmetic, operate(): jnp.stack([centre[0] - absorb * centre[1], centre[1] + absorb * centre[0]])  23.3 us
    all_to_all x1, blocking collectives, body(): lax.all_to_all(planes, ('group', 'dev'), split_axis=2, concat_axis=1, til...  14.8 us
    sub x1, other arithmetic, body(): residual = source - operate(padded, wavenumber_sq)  10.6 us
    dot_general x1, matrix products, body(): correction = jnp.einsum('cmxy,mz->cxyz', modes, basis, precision=HIGHEST)  10.1 us
    all_to_all x1, starting transfers between devices, body(): lax.all_to_all(flat, ('group', 'dev'), split_axis=1, concat_axis=2, tiled...  9.63 us
  transfers between devices with their start and end apart: 17, of which 1 were waited for; matrix products, arithmetic and copies ran while one was open for 13% of the time, Pallas kernels for 0%

commit v1 on v0

v1 whole, which is shorter than its diff:
```python
import functools
import math

import jax
import jax.numpy as jnp
import numpy as np
from jax import lax
from jax.experimental import pallas as pl
from jax.experimental.pallas import tpu as pltpu
from jax.sharding import PartitionSpec as P

SWEEPS = 3
RELAX = 0.8
DAMPING = 0.5
HIGHEST = lax.Precision.HIGHEST
MESH = pl.DeviceIdType.MESH

GROUPS, MEMBERS = 8, 16
DEVICES = GROUPS * MEMBERS
LX, LY, NZ = 64, 32, 256
CX, CY = LX // 4, LY // 4
PAD_X, PAD_Y = LX + 2, LY + 16
LANES = 128
TILES = LY // 8
F32 = jnp.float32


def block_real(matrix):
    return np.block([[matrix.real, -matrix.imag], [matrix.imag, matrix.real]])


def tables():
    count = 128
    z = np.arange(NZ) + 1
    basis = math.sqrt(2.0 / (NZ + 1)) * np.sin(math.pi / (NZ + 1) * np.outer(z, z))

    def dft(n):
        return np.exp(-2j * math.pi * np.outer(np.arange(n), np.arange(n)) / n)

    rows = np.kron(dft(GROUPS), dft(MEMBERS))
    lanes = np.kron(dft(CX), dft(CY))
    j1, k1 = np.repeat(np.arange(GROUPS), MEMBERS), np.tile(np.arange(MEMBERS), GROUPS)
    xi, yi = np.repeat(np.arange(CX), CY), np.tile(np.arange(CY), CX)
    twiddle = np.exp(-2j * math.pi * (np.outer(j1, xi) + np.outer(k1, yi)) / count)
    j2, k2 = xi, yi
    wave_x = j1[:, None] + GROUPS * j2[None, :]
    wave_y = k1[:, None] + MEMBERS * k2[None, :]
    eigen = (2 - 2 * np.cos(2 * math.pi * wave_x / count)) / 16
    eigen = eigen + (2 - 2 * np.cos(2 * math.pi * wave_y / count)) / 16
    vertical = 2 - 2 * np.cos(math.pi * z / (NZ + 1))
    forward_rows = block_real(rows)
    forward_lanes = block_real(lanes).T
    floats = (
        basis,
        forward_rows,
        forward_lanes,
        forward_lanes.T / count,
        forward_rows.T / count,
        np.stack([twiddle.real, twiddle.imag]),
        eigen,
        vertical,
    )
    return [np.asarray(a, np.float32) for a in floats]


def dot(a, b, contract):
    return lax.dot_general(
        a, b, ((contract[:1], contract[1:]), ((), ())), precision=HIGHEST,
        preferred_element_type=F32,
    )


def stencil(field, x, tile, absorb, lane):
    low = 8 + 8 * tile
    centre = [field[hc, x + 1, low : low + 8, :] for hc in range(4)]
    total = []
    for hc in range(4):
        beside = field[hc, x, low : low + 8, :] + field[hc, x + 2, low : low + 8, :]
        beside = beside + field[hc, x + 1, low - 1 : low + 7, :]
        beside = beside + field[hc, x + 1, low + 1 : low + 9, :]
        total.append(beside)
    after = [pltpu.roll(v, 1, axis=1) for v in centre]
    before = [pltpu.roll(v, LANES - 1, axis=1) for v in centre]
    robin = [
        centre[0] - absorb * centre[2],
        centre[1] - absorb * centre[3],
        centre[2] + absorb * centre[0],
        centre[3] + absorb * centre[1],
    ]
    first, final = lane == 0, lane == LANES - 1
    for c in range(2):
        a, b = 2 * c, 2 * c + 1
        total[a] = total[a] + jnp.where(first, robin[a], after[a])
        total[a] = total[a] + jnp.where(final, before[b], before[a])
        total[b] = total[b] + jnp.where(first, after[a], after[b])
        total[b] = total[b] + jnp.where(final, robin[b], before[b])
    return centre, total


def kernel(
    f_hbm, s_hbm, k_hbm, shift_ref, vertical_ref,
    basis_ref, rows_ref, lanes_ref, unlanes_ref, unrows_ref, twiddle_ref, eigen_ref,
    out_hbm,
    fa, fb, src, wave, weight, absorb_ref, summed, coarse,
    send1, recv1, send2, recv2,
    sy, sx, ry, rx, sey, sex, rey, rex,
    load_sem, store_sem, a2a_sem, halo_send, halo_recv,
):
    g, d = lax.axis_index("group"), lax.axis_index("dev")
    me = g * MEMBERS + d

    loads = []
    for c in range(2):
        for h in range(2):
            z = pl.ds(LANES * h, LANES)
            loads.append(pltpu.make_async_copy(
                f_hbm.at[c, :, :, z], fa.at[2 * c + h, pl.ds(1, LX), pl.ds(8, LY), :],
                load_sem.at[2 * c + h]))
    for c in range(2):
        for h in range(2):
            z = pl.ds(LANES * h, LANES)
            loads.append(pltpu.make_async_copy(
                s_hbm.at[c, :, :, z], src.at[2 * c + h], load_sem.at[4 + 2 * c + h]))
    for h in range(2):
        loads.append(pltpu.make_async_copy(
            k_hbm.at[:, :, pl.ds(LANES * h, LANES)], wave.at[h], load_sem.at[8 + h]))
    for copy in loads:
        copy.start()

    for ref in (ry, rx, rey, rex):
        ref[...] = jnp.zeros_like(ref)

    barrier = pltpu.get_barrier_semaphore()

    def greet(i, carry):
        t = lax.rem(me + i, DEVICES)
        pl.semaphore_signal(
            barrier, inc=1, device_id=(t // MEMBERS, lax.rem(t, MEMBERS)), device_id_type=MESH)
        return carry

    lax.fori_loop(1, DEVICES, greet, 0)

    for ref in (fa, fb):
        ref[:, 0] = jnp.zeros((4, PAD_Y, LANES), F32)
        ref[:, PAD_X - 1] = jnp.zeros((4, PAD_Y, LANES), F32)

        def clear(x, carry, ref=ref):
            ref[:, x, 0:8, :] = jnp.zeros((4, 8, LANES), F32)
            ref[:, x, PAD_Y - 8 : PAD_Y, :] = jnp.zeros((4, 8, LANES), F32)
            return carry

        lax.fori_loop(1, PAD_X - 1, clear, 0)

    pl.semaphore_wait(barrier, DEVICES - 1)

    def sides(e, out_y, out_x, in_y, in_x):
        plan = []
        for side in range(2):
            step = 2 * side - 1
            for axis, (place, size, out, into) in enumerate(
                ((d, MEMBERS, out_y, in_y), (g, GROUPS, out_x, in_x))
            ):
                here = place > 0 if side == 0 else place < size - 1
                target = (g, d + step) if axis == 0 else (g + step, d)
                plan.append((
                    here,
                    pltpu.make_async_remote_copy(
                        src_ref=out.at[side], dst_ref=into.at[1 - side],
                        send_sem=halo_send.at[e, 2 * axis + side],
                        recv_sem=halo_recv.at[e, 2 * axis + 1 - side],
                        device_id=target, device_id_type=MESH),
                    pltpu.make_async_remote_copy(
                        src_ref=out.at[side], dst_ref=into.at[side],
                        send_sem=halo_send.at[e, 2 * axis + side],
                        recv_sem=halo_recv.at[e, 2 * axis + side],
                        device_id=target, device_id_type=MESH),
                ))
        return plan

    def start_sides(plan):
        for here, copy, _ in plan:
            pl.when(here)(copy.start)

    def finish_sides(plan):
        for here, _, arrived in plan:
            @pl.when(here)
            def _(arrived=arrived):
                arrived.wait_send()
                arrived.wait_recv()

    def pack(field, e):
        flat = field.reshape(4, PAD_X * PAD_Y, LANES)
        for hc in range(4):
            for side, row in ((0, 8), (1, 7 + LY)):
                sy[e, side, hc] = flat[hc, pl.ds(PAD_Y + row, LX, stride=PAD_Y), :]
            for side, x in ((0, 1), (1, LX)):
                sx[e, side, hc] = field[hc, x, 8 : 8 + LY, :]

    def beside(e):
        return sides(e, sy.at[e], sx.at[e], ry.at[e], rx.at[e])

    for copy in loads[:4]:
        copy.wait()
    pack(fa, 0)
    start = beside(0)
    start_sides(start)
    for copy in loads[4:]:
        copy.wait()

    lane = lax.broadcasted_iota(jnp.int32, (8, LANES), 1)
    sub = lax.broadcasted_iota(jnp.int32, (8, LANES), 0)

    def residual(xi, carry):
        for tile in range(TILES):
            rows = slice(8 * tile, 8 * tile + 8)
            sums = [None] * 4
            for q in range(4):
                x = 4 * xi + q
                k = [wave[h, x, rows, :] for h in range(2)]
                absorb = jnp.sqrt(jnp.where(lane < LANES // 2, k[0], k[1]))
                absorb_ref[x, rows, :] = absorb
                diagonal = [6.0 - v for v in k]
                for h in range(2):
                    weight[h, x, rows, :] = RELAX / diagonal[h]
                centre, total = stencil(fa, x, tile, absorb, lane)
                for hc in range(4):
                    value = src[hc, x, rows, :] + total[hc] - diagonal[hc % 2] * centre[hc]
                    sums[hc] = value if q == 0 else sums[hc] + value
            for hc in range(4):
                summed[hc, pl.ds(pl.multiple_of(xi * LY + 8 * tile, 8), 8), :] = sums[hc]
        return carry

    lax.fori_loop(0, CX, residual, 0)

    finish_sides(start)
    cells = CX * CY
    for hc in range(4):
        value = summed[hc, pl.ds(0, cells, stride=4), :]
        for q in range(1, 4):
            value = value + summed[hc, pl.ds(q, cells, stride=4), :]
        coarse[hc] = value
        for side in range(2):
            for q in range(4):
                at = pl.ds(7 * side, CX, stride=CY)
                coarse[hc, at, :] = coarse[hc, at, :] + ry[0, side, hc, pl.ds(q, CX, stride=4), :]
            for q in range(4):
                at = pl.ds((CX - 1) * CY * side, CY)
                coarse[hc, at, :] = coarse[hc, at, :] + rx[0, side, hc, pl.ds(q, CY, stride=4), :]

    mean = jnp.concatenate(
        [jnp.concatenate([coarse[0], coarse[1]], axis=1),
         jnp.concatenate([coarse[2], coarse[3]], axis=1)], axis=0) * (1.0 / 16.0)
    modes = dot(basis_ref[...], mean, (1, 1))
    send1_flat = send1.reshape(4 * DEVICES, LANES)
    for m in range(2):
        for c in range(2):
            send1_flat[pl.ds(2 * m + c, DEVICES, stride=4), :] = modes[
                DEVICES * m : DEVICES * (m + 1), LANES * c : LANES * (c + 1)]

    def to_all(source, target, index):
        def one(i, carry):
            t = lax.rem(me + i, DEVICES)
            pltpu.make_async_remote_copy(
                src_ref=source.at[t], dst_ref=target.at[me],
                send_sem=a2a_sem.at[2 * index], recv_sem=a2a_sem.at[2 * index + 1],
                device_id=(t // MEMBERS, lax.rem(t, MEMBERS)), device_id_type=MESH).start()
            return carry

        lax.fori_loop(1, DEVICES, one, 0)
        target[me] = source[me]
        some = pl.ds(0, DEVICES - 1)
        pltpu.make_async_copy(source.at[some], source.at[some], a2a_sem.at[2 * index]).wait()
        pltpu.make_async_copy(target.at[some], target.at[some], a2a_sem.at[2 * index + 1]).wait()

    to_all(send1, recv1, 0)

    recv1_flat = recv1.reshape(4 * DEVICES, LANES)
    part = [recv1_flat[pl.ds(q, DEVICES, stride=4), :] for q in range(4)]
    planes = jnp.concatenate(
        [jnp.concatenate([part[0], part[2]], axis=1),
         jnp.concatenate([part[1], part[3]], axis=1)], axis=0)
    planes = dot(rows_ref[...], planes, (1, 0))
    cosine, sine = twiddle_ref[0], twiddle_ref[1]

    def quarter(value, row, column):
        return value[LANES * row : LANES * (row + 1), LANES * column : LANES * (column + 1)]

    turned = []
    for m in range(2):
        real, imag = quarter(planes, 0, m), quarter(planes, 1, m)
        turned.append(jnp.concatenate(
            [real * cosine - imag * sine, real * sine + imag * cosine], axis=1))
    planes = dot(jnp.concatenate(turned, axis=0), lanes_ref[...], (1, 0))
    shift = shift_ref[0]
    imag_part = -DAMPING * shift
    solved = []
    for m in range(2):
        real, imag = quarter(planes, m, 0), quarter(planes, m, 1)
        real_part = eigen_ref[...] + (vertical_ref[me + DEVICES * m] - shift)
        modulus = real_part * real_part + imag_part * imag_part
        upper = (real * real_part + imag * imag_part) / modulus
        lower = (imag * real_part - real * imag_part) / modulus
        solved.append(jnp.concatenate([upper, lower], axis=1))
    planes = dot(jnp.concatenate(solved, axis=0), unlanes_ref[...], (1, 0))
    turned = [[], []]
    for m in range(2):
        real, imag = quarter(planes, m, 0), quarter(planes, m, 1)
        turned[0].append(real * cosine + imag * sine)
        turned[1].append(imag * cosine - real * sine)
    planes = dot(
        unrows_ref[...],
        jnp.concatenate([jnp.concatenate(row, axis=1) for row in turned], axis=0), (1, 0))
    send2_flat = send2.reshape(4 * DEVICES, LANES)
    for m in range(2):
        for c in range(2):
            send2_flat[pl.ds(2 * m + c, DEVICES, stride=4), :] = quarter(planes, c, m)

    to_all(send2, recv2, 1)

    recv2_flat = recv2.reshape(4 * DEVICES, LANES)
    part = [recv2_flat[pl.ds(q, DEVICES, stride=4), :] for q in range(4)]
    modes = jnp.concatenate(
        [jnp.concatenate([part[0], part[1]], axis=1),
         jnp.concatenate([part[2], part[3]], axis=1)], axis=0)
    correction = dot(modes, basis_ref[...], (0, 0))
    for c in range(2):
        for h in range(2):
            coarse[2 * c + h] = quarter(correction, c, h)

    for hc in range(4):
        for side in range(2):
            sey[side, hc] = coarse[hc, pl.ds(7 * side, CX, stride=CY), :]
            sex[side, hc] = coarse[hc, pl.ds((CX - 1) * CY * side, CY), :]
    edges = sides(3, sey, sex, rey, rex)
    start_sides(edges)

    def prolong(xi, carry):
        for tile in range(TILES):
            row = xi * CY + 2 * tile
            for hc in range(4):
                lower = jnp.broadcast_to(coarse[hc, pl.ds(row, 1), :], (8, LANES))
                upper = jnp.broadcast_to(coarse[hc, pl.ds(row + 1, 1), :], (8, LANES))
                spread = jnp.where(sub < 4, lower, upper)
                for q in range(4):
                    x = 4 * xi + q + 1
                    at = slice(8 + 8 * tile, 16 + 8 * tile)
                    fa[hc, x, at, :] = fa[hc, x, at, :] + spread
        return carry

    lax.fori_loop(0, CX, prolong, 0)

    def sweep(old, new):
        def one(x, carry):
            for tile in range(TILES):
                rows = slice(8 * tile, 8 * tile + 8)
                centre, total = stencil(old, x, tile, absorb_ref[x, rows, :], lane)
                for hc in range(4):
                    value = weight[hc % 2, x, rows, :] * (src[hc, x, rows, :] + total[hc])
                    new[hc, x + 1, 8 + 8 * tile : 16 + 8 * tile, :] = (
                        (1.0 - RELAX) * centre[hc] + value)
            return carry

        lax.fori_loop(0, LX, one, 0)

    def add_halos(new, e):
        flat = new.reshape(4, PAD_X * PAD_Y, LANES)
        scale = weight.reshape(2, LX * LY, LANES)
        for hc in range(4):
            h = hc % 2
            for side, row in ((0, 0), (1, LY - 1)):
                at = pl.ds(PAD_Y + 8 + row, LX, stride=PAD_Y)
                flat[hc, at, :] = flat[hc, at, :] + (
                    scale[h, pl.ds(row, LX, stride=LY), :] * ry[e, side, hc])
            for side, x in ((0, 0), (1, LX - 1)):
                new[hc, x + 1, 8 : 8 + LY, :] = new[hc, x + 1, 8 : 8 + LY, :] + (
                    weight[h, x] * rx[e, side, hc])

    sweep(fa, fb)
    finish_sides(edges)
    for hc in range(4):
        for side in range(2):
            for q in range(4):
                at = pl.ds(q, CX, stride=4)
                ry[0, side, hc, at, :] = ry[0, side, hc, at, :] + rey[side, hc]
                at = pl.ds(q, CY, stride=4)
                rx[0, side, hc, at, :] = rx[0, side, hc, at, :] + rex[side, hc]
    add_halos(fb, 0)
    for e, old, new in ((1, fb, fa), (2, fa, fb)):
        pack(old, e)
        plan = beside(e)
        start_sides(plan)
        sweep(old, new)
        finish_sides(plan)
        add_halos(new, e)

    stores = []
    for c in range(2):
        for h in range(2):
            stores.append(pltpu.make_async_copy(
                fb.at[2 * c + h, pl.ds(1, LX), pl.ds(8, LY), :],
                out_hbm.at[c, :, :, pl.ds(LANES * h, LANES)], store_sem.at[2 * c + h]))
    for copy in stores:
        copy.start()
    for copy in stores:
        copy.wait()


def body(field_now, source, wavenumber_sq, shift_sq):
    basis, rows, lanes, unlanes, unrows, twiddle, eigen, vertical = tables()
    anywhere = pl.BlockSpec(memory_space=pl.ANY)
    scalars = pl.BlockSpec(memory_space=pltpu.SMEM)
    whole = pl.BlockSpec(memory_space=pltpu.VMEM)
    vmem = pltpu.VMEM
    dma = pltpu.SemaphoreType.DMA
    return pl.pallas_call(
        kernel,
        out_shape=jax.ShapeDtypeStruct(field_now.shape, F32),
        in_specs=[anywhere] * 3 + [scalars] * 2 + [whole] * 7,
        out_specs=anywhere,
        scratch_shapes=[
            vmem((4, PAD_X, PAD_Y, LANES), F32),
            vmem((4, PAD_X, PAD_Y, LANES), F32),
            vmem((4, LX, LY, LANES), F32),
            vmem((2, LX, LY, LANES), F32),
            vmem((2, LX, LY, LANES), F32),
            vmem((LX, LY, LANES), F32),
            vmem((4, CX * LY, LANES), F32),
            vmem((4, CX * CY, LANES), F32),
            vmem((DEVICES, 4, LANES), F32),
            vmem((DEVICES, 4, LANES), F32),
            vmem((DEVICES, 4, LANES), F32),
            vmem((DEVICES, 4, LANES), F32),
            vmem((3, 2, 4, LX, LANES), F32),
            vmem((3, 2, 4, LY, LANES), F32),
            vmem((3, 2, 4, LX, LANES), F32),
            vmem((3, 2, 4, LY, LANES), F32),
            vmem((2, 4, CX, LANES), F32),
            vmem((2, 4, CY, LANES), F32),
            vmem((2, 4, CX, LANES), F32),
            vmem((2, 4, CY, LANES), F32),
            dma((10,)),
            dma((4,)),
            dma((4,)),
            dma((4, 4)),
            dma((4, 4)),
        ],
        compiler_params=pltpu.CompilerParams(
            collective_id=0, has_side_effects=True, vmem_limit_bytes=48 << 20),
        name="schwarz",
    )(field_now, source, wavenumber_sq, shift_sq, vertical,
      basis, rows, lanes, unlanes, unrows, twiddle, eigen)


def solution(mesh):
    return jax.shard_map(
        body,
        mesh=mesh,
        in_specs=(
            P(None, "group", "dev", None),
            P(None, "group", "dev", None),
            P("group", "dev", None),
            P(),
        ),
        out_specs=P(None, "group", "dev", None),
        check_vma=False,
    )
```

time: 251 us -> 77.6 us (0.31)
  the two profiles are of different devices: /device:TPU:25 before, /device:TPU:1 now
where the time goes in v1:
time: 77.6 us; the launch traced here: 77.2 us
  Pallas kernels  63 us (81%)
  local copies, waits for them, and re-layouts  13.5 us (17%)
    pallas_call x1, Pallas kernels, body(): pl.pallas_call(kernel, out_shape=jax.ShapeDtypeStruct(field_now.shape, F3...  63 us
    unnamed x19, local copies, waits for them, and re-layouts  13.5 us

profile of v1, /device:TPU:1, one launch (start us, length us, event | category | flops | bytes accessed | tf_op | source)
XLA Modules:
  0.0 77.2 jit_solution(12620937362186889796)
XLA Ops:
  0.7 0.0 copy-start
  0.7 1.6 %copy-done = f32[64,32,256]{2,1,0:T(8,128)S(1)} copy-done((f32[64,32,256]{2,1,0:T(8,128)S(1)}, f32[64,32,256]{2,1,0:T(8,128)}, u32[]{:S(2)}) %copy-start) | copy-done | bytes 2097176
  2.2 0.0 copy-start.1
  2.2 0.9 %copy-done.1 = f32[256,256]{1,0:T(8,128)S(1)} copy-done((f32[256,256]{1,0:T(8,128)S(1)}, f32[256,256]{1,0:T(8,128)}, u32[]{:S(2)}) %copy-start.1) | copy-done | bytes 262168
  3.2 0.0 copy-start.2
  3.2 0.9 %copy-done.2 = f32[256,256]{1,0:T(8,128)S(1)} copy-done((f32[256,256]{1,0:T(8,128)S(1)}, f32[256,256]{1,0:T(8,128)}, u32[]{:S(2)}) %copy-start.2) | copy-done | bytes 262168
  4.1 0.0 copy-start.3
  4.1 0.9 %copy-done.3 = f32[256,256]{1,0:T(8,128)S(1)} copy-done((f32[256,256]{1,0:T(8,128)S(1)}, f32[256,256]{1,0:T(8,128)}, u32[]{:S(2)}) %copy-start.3) | copy-done | bytes 262168
  5.1 0.0 copy-start.4
  5.1 0.9 %copy-done.4 = f32[256,256]{1,0:T(8,128)S(1)} copy-done((f32[256,256]{1,0:T(8,128)S(1)}, f32[256,256]{1,0:T(8,128)}, u32[]{:S(2)}) %copy-start.4) | copy-done | bytes 262168
  6.0 0.0 copy-start.5
  6.0 0.9 %copy-done.5 = f32[256,256]{1,0:T(8,128)S(1)} copy-done((f32[256,256]{1,0:T(8,128)S(1)}, f32[256,256]{1,0:T(8,128)}, u32[]{:S(2)}) %copy-start.5) | copy-done | bytes 262168
  7.0 0.0 copy-start.6
  7.0 0.9 %copy-done.6 = f32[2,128,128]{2,1,0:T(8,128)S(1)} copy-done((f32[2,128,128]{2,1,0:T(8,128)S(1)}, f32[2,128,128]{2,1,0:T(8,128)}, u32[]{:S(2)}) %copy-start.6) | copy-done | bytes 131096
  7.9 0.0 copy-start.7
  7.9 0.8 %copy-done.7 = f32[128,128]{1,0:T(8,128)S(1)} copy-done((f32[128,128]{1,0:T(8,128)S(1)}, f32[128,128]{1,0:T(8,128)}, u32[]{:S(2)}) %copy-start.7) | copy-done | bytes 65560
  8.7 0.0 copy-start.8
  8.7 0.7 copy-done.8
  9.4 63.0 %schwarz.1 = f32[2,64,32,256]{3,2,1,0:T(8,128)} custom-call(f32[2,64,32,256]{3,2,1,0:T(8,128)} %f_hbm.1, f32[2,64,32,256]{3,2,1,0:T(8,128)} %s_hbm.1, f32[64,32,256]{2,1,0:T(8,128)S(1)} %copy-done, f32[1]{0:T(128)S(6)} %copy.14.shift_ref, f32[256]{0:T(256)S(1)} %copy-done.8, f32[256,256]{1,0:T(8,128)S(1)} %copy-done.5, f32[256,256]{1,0:T(8,128)S(1)} %copy-done.4, ...), custom_call_target="tpu_custom_call" | custom-call | tf_op jit(solution)/shard_map/schwarz/pallas_call | solution.py:415
  72.4 4.8 %copy.15 = f32[2,64,32,256]{3,2,1,0:T(8,128)} copy(f32[2,64,32,256]{3,2,1,0:T(8,128)} %schwarz.1) | data formatting | bytes 8388608
Async XLA Ops:
  0.7 1.6 %copy-start = (f32[64,32,256]{2,1,0:T(8,128)S(1)}, f32[64,32,256]{2,1,0:T(8,128)}, u32[]{:S(2)}) copy-start(f32[64,32,256]{2,1,0:T(8,128)} %k_hbm.1) | copy-start | bytes 6291460
  2.2 0.9 %copy-start.1 = (f32[256,256]{1,0:T(8,128)S(1)}, f32[256,256]{1,0:T(8,128)}, u32[]{:S(2)}) copy-start(f32[256,256]{1,0:T(8,128)} %constant.21.clone.unrows_ref) | copy-start | bytes 786436
  3.2 0.9 %copy-start.2 = (f32[256,256]{1,0:T(8,128)S(1)}, f32[256,256]{1,0:T(8,128)}, u32[]{:S(2)}) copy-start(f32[256,256]{1,0:T(8,128)} %constant.20.clone.unlanes_ref) | copy-start | bytes 786436
  4.1 0.9 %copy-start.3 = (f32[256,256]{1,0:T(8,128)S(1)}, f32[256,256]{1,0:T(8,128)}, u32[]{:S(2)}) copy-start(f32[256,256]{1,0:T(8,128)} %constant.19.clone.lanes_ref) | copy-start | bytes 786436
  5.1 0.9 %copy-start.4 = (f32[256,256]{1,0:T(8,128)S(1)}, f32[256,256]{1,0:T(8,128)}, u32[]{:S(2)}) copy-start(f32[256,256]{1,0:T(8,128)} %constant.18.clone.rows_ref) | copy-start | bytes 786436
  6.0 0.9 %copy-start.5 = (f32[256,256]{1,0:T(8,128)S(1)}, f32[256,256]{1,0:T(8,128)}, u32[]{:S(2)}) copy-start(f32[256,256]{1,0:T(8,128)} %constant.17.clone.basis_ref) | copy-start | bytes 786436
  7.0 0.9 %copy-start.6 = (f32[2,128,128]{2,1,0:T(8,128)S(1)}, f32[2,128,128]{2,1,0:T(8,128)}, u32[]{:S(2)}) copy-start(f32[2,128,128]{2,1,0:T(8,128)} %constant.22.clone.twiddle_ref) | copy-start | bytes 393220
  7.9 0.8 %copy-start.7 = (f32[128,128]{1,0:T(8,128)S(1)}, f32[128,128]{1,0:T(8,128)}, u32[]{:S(2)}) copy-start(f32[128,128]{1,0:T(8,128)} %constant.23.clone.eigen_ref) | copy-start | bytes 196612
  8.7 0.7 copy-start.8

commit v2 on v1

--- a/solution.py
+++ b/solution.py
@@ -10,6 +10,8 @@
 from jax.sharding import PartitionSpec as P
 
 SWEEPS = 3
+UNROLL = 4
+LIMIT = 67043328
 RELAX = 0.8
 DAMPING = 0.5
 HIGHEST = lax.Precision.HIGHEST
@@ -19,6 +21,7 @@
 DEVICES = GROUPS * MEMBERS
 LX, LY, NZ = 64, 32, 256
 CX, CY = LX // 4, LY // 4
+PARTS = 4
 PAD_X, PAD_Y = LX + 2, LY + 16
 LANES = 128
 TILES = LY // 8
@@ -50,17 +53,9 @@
     vertical = 2 - 2 * np.cos(math.pi * z / (NZ + 1))
     forward_rows = block_real(rows)
     forward_lanes = block_real(lanes).T
-    floats = (
-        basis,
-        forward_rows,
-        forward_lanes,
-        forward_lanes.T / count,
-        forward_rows.T / count,
-        np.stack([twiddle.real, twiddle.imag]),
-        eigen,
-        vertical,
-    )
-    return [np.asarray(a, np.float32) for a in floats]
+    wide = [basis, forward_rows, forward_lanes, forward_lanes.T / count, forward_rows.T / count]
+    narrow = [twiddle.real, twiddle.imag, eigen, np.tile(vertical[:, None], (1, LANES))]
+    return np.float32(np.stack(wide)), np.float32(np.concatenate(narrow))
 
 
 def dot(a, b, contract):
@@ -98,47 +93,69 @@
 
 
 def kernel(
-    f_hbm, s_hbm, k_hbm, shift_ref, vertical_ref,
-    basis_ref, rows_ref, lanes_ref, unlanes_ref, unrows_ref, twiddle_ref, eigen_ref,
-    out_hbm,
-    fa, fb, src, wave, weight, absorb_ref, summed, coarse,
+    f_hbm, s_hbm, k_hbm, shift_ref, wide_hbm, narrow_hbm,
+    out_hbm, edge_y_hbm, edge_x_hbm,
+    fa, fb, res, edge_y, edge_x, src, wave, weight, absorb_ref, summed, coarse, wide, narrow,
     send1, recv1, send2, recv2,
     sy, sx, ry, rx, sey, sex, rey, rex,
-    load_sem, store_sem, a2a_sem, halo_send, halo_recv,
+    load_sem, part_sem, table_sem, a2a_sem, halo_send, halo_recv, store_sem, ready,
 ):
     g, d = lax.axis_index("group"), lax.axis_index("dev")
     me = g * MEMBERS + d
 
+    barrier = pltpu.get_barrier_semaphore()
+
+    column = [lax.rem(d + j, MEMBERS) for j in range(MEMBERS)]
+
+    def everyone(start):
+        def row(i, carry):
+            tg = lax.rem(g + i, GROUPS)
+            for td in column:
+                start(tg, td)
+            return carry
+
+        lax.fori_loop(1, GROUPS, row, 0)
+        for td in column[1:]:
+            start(g, td)
+
+    for ref in (ry, rx, rey, rex):
+        ref[...] = jnp.zeros_like(ref)
+
+    for i in range(1, GROUPS):
+        pl.semaphore_signal(
+            barrier, inc=1, device_id=(lax.rem(g + i, GROUPS), d), device_id_type=MESH)
+    for td in column[1:]:
+        pl.semaphore_signal(barrier, inc=1, device_id=(g, td), device_id_type=MESH)
+
+    halves = [pl.ds(LANES * h, LANES) for h in range(2)]
     loads = []
-    for c in range(2):
-        for h in range(2):
-            z = pl.ds(LANES * h, LANES)
-            loads.append(pltpu.make_async_copy(
-                f_hbm.at[c, :, :, z], fa.at[2 * c + h, pl.ds(1, LX), pl.ds(8, LY), :],
-                load_sem.at[2 * c + h]))
-    for c in range(2):
-        for h in range(2):
-            z = pl.ds(LANES * h, LANES)
-            loads.append(pltpu.make_async_copy(
-                s_hbm.at[c, :, :, z], src.at[2 * c + h], load_sem.at[4 + 2 * c + h]))
-    for h in range(2):
+    for hc in range(4):
         loads.append(pltpu.make_async_copy(
-            k_hbm.at[:, :, pl.ds(LANES * h, LANES)], wave.at[h], load_sem.at[8 + h]))
+            f_hbm.at[hc // 2, :, :, halves[hc % 2]],
+            fa.at[hc, pl.ds(1, LX), pl.ds(8, LY), :], load_sem.at[hc]))
     for copy in loads:
         copy.start()
 
-    for ref in (ry, rx, rey, rex):
-        ref[...] = jnp.zeros_like(ref)
-
-    barrier = pltpu.get_barrier_semaphore()
-
-    def greet(i, carry):
-        t = lax.rem(me + i, DEVICES)
-        pl.semaphore_signal(
-            barrier, inc=1, device_id=(t // MEMBERS, lax.rem(t, MEMBERS)), device_id_type=MESH)
-        return carry
-
-    lax.fori_loop(1, DEVICES, greet, 0)
+    def part_loads(i):
+        x = pl.ds(i * (LX // PARTS), LX // PARTS)
+        copies = []
+        for hc in range(4):
+            copies.append(pltpu.make_async_copy(
+                s_hbm.at[hc // 2, x, :, halves[hc % 2]], src.at[hc, x], part_sem.at[i, hc]))
+        for h in range(2):
+            copies.append(pltpu.make_async_copy(
+                k_hbm.at[x, :, halves[h]], wave.at[h, x], part_sem.at[i, 4 + h]))
+        return copies
+
+    for i in range(PARTS):
+        for copy in part_loads(i):
+            copy.start()
+    constants = [
+        pltpu.make_async_copy(wide_hbm, wide, table_sem.at[0]),
+        pltpu.make_async_copy(narrow_hbm, narrow, table_sem.at[1]),
+    ]
+    for copy in constants:
+        copy.start()
 
     for ref in (fa, fb):
         ref[:, 0] = jnp.zeros((4, PAD_Y, LANES), F32)
@@ -151,7 +168,10 @@
 
         lax.fori_loop(1, PAD_X - 1, clear, 0)
 
-    pl.semaphore_wait(barrier, DEVICES - 1)
+    pl.semaphore_wait(barrier, GROUPS + MEMBERS - 2)
+    for i in range(1, GROUPS):
+        pl.semaphore_signal(
+            ready, inc=1, device_id=(lax.rem(g + i, GROUPS), d), device_id_type=MESH)
 
     def sides(e, out_y, out_x, in_y, in_x):
         plan = []
@@ -199,13 +219,11 @@
     def beside(e):
         return sides(e, sy.at[e], sx.at[e], ry.at[e], rx.at[e])
 
-    for copy in loads[:4]:
+    for copy in loads:
         copy.wait()
     pack(fa, 0)
     start = beside(0)
     start_sides(start)
-    for copy in loads[4:]:
-        copy.wait()
 
     lane = lax.broadcasted_iota(jnp.int32, (8, LANES), 1)
     sub = lax.broadcasted_iota(jnp.int32, (8, LANES), 0)
@@ -230,7 +248,14 @@
                 summed[hc, pl.ds(pl.multiple_of(xi * LY + 8 * tile, 8), 8), :] = sums[hc]
         return carry
 
-    lax.fori_loop(0, CX, residual, 0)
+    def residual_part(i, carry):
+        for copy in part_loads(i):
+            copy.wait()
+        return lax.fori_loop(i * (CX // PARTS), (i + 1) * (CX // PARTS), residual, carry)
+
+    lax.fori_loop(0, PARTS, residual_part, 0)
+    for copy in constants:
+        copy.wait()
 
     finish_sides(start)
     cells = CX * CY
@@ -250,7 +275,7 @@
     mean = jnp.concatenate(
         [jnp.concatenate([coarse[0], coarse[1]], axis=1),
          jnp.concatenate([coarse[2], coarse[3]], axis=1)], axis=0) * (1.0 / 16.0)
-    modes = dot(basis_ref[...], mean, (1, 1))
+    modes = dot(wide[0], mean, (1, 1))
     send1_flat = send1.reshape(4 * DEVICES, LANES)
     for m in range(2):
         for c in range(2):
@@ -258,20 +283,20 @@
                 DEVICES * m : DEVICES * (m + 1), LANES * c : LANES * (c + 1)]
 
     def to_all(source, target, index):
-        def one(i, carry):
-            t = lax.rem(me + i, DEVICES)
+
+        def one(tg, td):
             pltpu.make_async_remote_copy(
-                src_ref=source.at[t], dst_ref=target.at[me],
+                src_ref=source.at[tg * MEMBERS + td], dst_ref=target.at[me],
                 send_sem=a2a_sem.at[2 * index], recv_sem=a2a_sem.at[2 * index + 1],
-                device_id=(t // MEMBERS, lax.rem(t, MEMBERS)), device_id_type=MESH).start()
-            return carry
-
-        lax.fori_loop(1, DEVICES, one, 0)
+                device_id=(tg, td), device_id_type=MESH).start()
+
+        everyone(one)
         target[me] = source[me]
         some = pl.ds(0, DEVICES - 1)
         pltpu.make_async_copy(source.at[some], source.at[some], a2a_sem.at[2 * index]).wait()
         pltpu.make_async_copy(target.at[some], target.at[some], a2a_sem.at[2 * index + 1]).wait()
 
+    pl.semaphore_wait(ready, GROUPS - 1)
     to_all(send1, recv1, 0)
 
     recv1_flat = recv1.reshape(4 * DEVICES, LANES)
@@ -279,8 +304,8 @@
     planes = jnp.concatenate(
         [jnp.concatenate([part[0], part[2]], axis=1),
          jnp.concatenate([part[1], part[3]], axis=1)], axis=0)
-    planes = dot(rows_ref[...], planes, (1, 0))
-    cosine, sine = twiddle_ref[0], twiddle_ref[1]
+    planes = dot(wide[1], planes, (1, 0))
+    cosine, sine = narrow[0:LANES], narrow[LANES : 2 * LANES]
 
     def quarter(value, row, column):
         return value[LANES * row : LANES * (row + 1), LANES * column : LANES * (column + 1)]
@@ -290,25 +315,26 @@
         real, imag = quarter(planes, 0, m), quarter(planes, 1, m)
         turned.append(jnp.concatenate(
             [real * cosine - imag * sine, real * sine + imag * cosine], axis=1))
-    planes = dot(jnp.concatenate(turned, axis=0), lanes_ref[...], (1, 0))
+    planes = dot(jnp.concatenate(turned, axis=0), wide[2], (1, 0))
     shift = shift_ref[0]
     imag_part = -DAMPING * shift
     solved = []
     for m in range(2):
         real, imag = quarter(planes, m, 0), quarter(planes, m, 1)
-        real_part = eigen_ref[...] + (vertical_ref[me + DEVICES * m] - shift)
+        height = narrow[pl.ds(3 * LANES + me + DEVICES * m, 1), :]
+        real_part = narrow[2 * LANES : 3 * LANES] + (height - shift)
         modulus = real_part * real_part + imag_part * imag_part
         upper = (real * real_part + imag * imag_part) / modulus
         lower = (imag * real_part - real * imag_part) / modulus
         solved.append(jnp.concatenate([upper, lower], axis=1))
-    planes = dot(jnp.concatenate(solved, axis=0), unlanes_ref[...], (1, 0))
+    planes = dot(jnp.concatenate(solved, axis=0), wide[3], (1, 0))
     turned = [[], []]
     for m in range(2):
         real, imag = quarter(planes, m, 0), quarter(planes, m, 1)
         turned[0].append(real * cosine + imag * sine)
         turned[1].append(imag * cosine - real * sine)
     planes = dot(
-        unrows_ref[...],
+        wide[4],
         jnp.concatenate([jnp.concatenate(row, axis=1) for row in turned], axis=0), (1, 0))
     send2_flat = send2.reshape(4 * DEVICES, LANES)
     for m in range(2):
@@ -322,7 +348,7 @@
     modes = jnp.concatenate(
         [jnp.concatenate([part[0], part[1]], axis=1),
          jnp.concatenate([part[2], part[3]], axis=1)], axis=0)
-    correction = dot(modes, basis_ref[...], (0, 0))
+    correction = dot(modes, wide[0], (0, 0))
     for c in range(2):
         for h in range(2):
             coarse[2 * c + h] = quarter(correction, c, h)
@@ -349,18 +375,48 @@
 
     lax.fori_loop(0, CX, prolong, 0)
 
-    def sweep(old, new):
-        def one(x, carry):
+    def sweep(old, put, after=None):
+        def some(i, carry):
             for tile in range(TILES):
                 rows = slice(8 * tile, 8 * tile + 8)
-                centre, total = stencil(old, x, tile, absorb_ref[x, rows, :], lane)
-                for hc in range(4):
-                    value = weight[hc % 2, x, rows, :] * (src[hc, x, rows, :] + total[hc])
-                    new[hc, x + 1, 8 + 8 * tile : 16 + 8 * tile, :] = (
-                        (1.0 - RELAX) * centre[hc] + value)
+                results = []
+                for u in range(UNROLL):
+                    x = UNROLL * i + u
+                    centre, total = stencil(old, x, tile, absorb_ref[x, rows, :], lane)
+                    for hc in range(4):
+                        value = weight[hc % 2, x, rows, :] * (src[hc, x, rows, :] + total[hc])
+                        results.append((hc, x, (1.0 - RELAX) * centre[hc] + value))
+                for hc, x, value in results:
+                    put(hc, x, tile, value)
             return carry
 
-        lax.fori_loop(0, LX, one, 0)
+        steps = LX // UNROLL // PARTS
+
+        def part(i, carry):
+            lax.fori_loop(i * steps, (i + 1) * steps, some, carry)
+            if after is not None:
+                after(i)
+            return carry
+
+        lax.fori_loop(0, PARTS, part, 0)
+
+    def into(field):
+        def put(hc, x, tile, value):
+            field[hc, x + 1, 8 + 8 * tile : 16 + 8 * tile, :] = value
+
+        return put
+
+    def put_out(hc, x, tile, value):
+        res[hc, x, 8 * tile : 8 * tile + 8, :] = value
+
+    def stores(i):
+        x = pl.ds(i * (LX // PARTS), LX // PARTS)
+        return [pltpu.make_async_copy(res.at[hc, x], out_hbm.at[hc, x], store_sem.at[i, hc])
+                for hc in range(4)]
+
+    def start_stores(i):
+        for copy in stores(i):
+            copy.start()
 
     def add_halos(new, e):
         flat = new.reshape(4, PAD_X * PAD_Y, LANES)
@@ -375,7 +431,7 @@
                 new[hc, x + 1, 8 : 8 + LY, :] = new[hc, x + 1, 8 : 8 + LY, :] + (
                     weight[h, x] * rx[e, side, hc])
 
-    sweep(fa, fb)
+    sweep(fa, into(fb))
     finish_sides(edges)
     for hc in range(4):
         for side in range(2):
@@ -385,51 +441,100 @@
                 at = pl.ds(q, CY, stride=4)
                 rx[0, side, hc, at, :] = rx[0, side, hc, at, :] + rex[side, hc]
     add_halos(fb, 0)
-    for e, old, new in ((1, fb, fa), (2, fa, fb)):
-        pack(old, e)
-        plan = beside(e)
-        start_sides(plan)
-        sweep(old, new)
-        finish_sides(plan)
-        add_halos(new, e)
-
-    stores = []
-    for c in range(2):
-        for h in range(2):
-            stores.append(pltpu.make_async_copy(
-                fb.at[2 * c + h, pl.ds(1, LX), pl.ds(8, LY), :],
-                out_hbm.at[c, :, :, pl.ds(LANES * h, LANES)], store_sem.at[2 * c + h]))
-    for copy in stores:
+    pack(fb, 1)
+    plan = beside(1)
+    start_sides(plan)
+    sweep(fb, into(fa))
+    finish_sides(plan)
+    add_halos(fa, 1)
+    pack(fa, 2)
+    plan = beside(2)
+    start_sides(plan)
+    sweep(fa, put_out, start_stores)
+    finish_sides(plan)
+    scale = weight.reshape(2, LX * LY, LANES)
+    for hc in range(4):
+        h = hc % 2
+        for side, row in ((0, 0), (1, LY - 1)):
+            edge_y[side, hc] = scale[h, pl.ds(row, LX, stride=LY), :] * ry[2, side, hc]
+        for side, x in ((0, 0), (1, LX - 1)):
+            edge_x[side, hc] = weight[h, x] * rx[2, side, hc]
+    last = [
+        pltpu.make_async_copy(edge_y, edge_y_hbm, table_sem.at[0]),
+        pltpu.make_async_copy(edge_x, edge_x_hbm, table_sem.at[1]),
+    ]
+    for copy in last:
         copy.start()
-    for copy in stores:
+    for i in range(PARTS):
+        for copy in stores(i):
+            copy.wait()
+    for copy in last:
         copy.wait()
 
 
+def finish(parts, edge_y_hbm, edge_x_hbm, out_hbm, field, edge_y, edge_x, sem_in, sem_edge, sem_out):
+    edges = [
+        pltpu.make_async_copy(edge_y_hbm, edge_y, sem_edge.at[0]),
+        pltpu.make_async_copy(edge_x_hbm, edge_x, sem_edge.at[1]),
+    ]
+    half = LX // 2
+    blocks = [(hc, i) for hc in range(4) for i in range(2)]
+    loads = [
+        pltpu.make_async_copy(
+            parts.at[hc, pl.ds(half * i, half)], field.at[hc, pl.ds(half * i, half)],
+            sem_in.at[hc, i])
+        for hc, i in blocks
+    ]
+    stores = [
+        pltpu.make_async_copy(
+            field.at[hc, pl.ds(half * i, half)],
+            out_hbm.at[hc // 2, pl.ds(half * i, half), :, pl.ds(LANES * (hc % 2), LANES)],
+            sem_out.at[hc, i])
+        for hc, i in blocks
+    ]
+    for copy in edges + loads:
+        copy.start()
+    for copy in edges:
+        copy.wait()
+    flat = field.reshape(4, LX * LY, LANES)
+    for (hc, i), load, store in zip(blocks, loads, stores):
+        load.wait()
+        for side, row in ((0, 0), (1, LY - 1)):
+            at = pl.ds(half * i * LY + row, half, stride=LY)
+            flat[hc, at, :] = flat[hc, at, :] + edge_y[side, hc, half * i : half * (i + 1), :]
+        x = (LX - 1) * i
+        field[hc, x] = field[hc, x] + edge_x[i, hc]
+        store.start()
+    for store in stores:
+        store.wait()
+
+
 def body(field_now, source, wavenumber_sq, shift_sq):
-    basis, rows, lanes, unlanes, unrows, twiddle, eigen, vertical = tables()
-    anywhere = pl.BlockSpec(memory_space=pl.ANY)
-    scalars = pl.BlockSpec(memory_space=pltpu.SMEM)
-    whole = pl.BlockSpec(memory_space=pltpu.VMEM)
+    wide, narrow = tables()
+    hbm = pl.BlockSpec(memory_space=pltpu.HBM)
     vmem = pltpu.VMEM
     dma = pltpu.SemaphoreType.DMA
-    return pl.pallas_call(
+    edges = [(2, 4, LX, LANES), (2, 4, LY, LANES)]
+    parts = pl.pallas_call(
         kernel,
-        out_shape=jax.ShapeDtypeStruct(field_now.shape, F32),
-        in_specs=[anywhere] * 3 + [scalars] * 2 + [whole] * 7,
-        out_specs=anywhere,
+        out_shape=[jax.ShapeDtypeStruct(s, F32) for s in [(4, LX, LY, LANES)] + edges],
+        in_specs=[hbm] * 3 + [pl.BlockSpec(memory_space=pltpu.SMEM)] + [hbm] * 2,
+        out_specs=[hbm] * 3,
         scratch_shapes=[
             vmem((4, PAD_X, PAD_Y, LANES), F32),
             vmem((4, PAD_X, PAD_Y, LANES), F32),
+            vmem((4, LX, LY, LANES), F32),
+            vmem(edges[0], F32),
+            vmem(edges[1], F32),
             vmem((4, LX, LY, LANES), F32),
             vmem((2, LX, LY, LANES), F32),
             vmem((2, LX, LY, LANES), F32),
             vmem((LX, LY, LANES), F32),
             vmem((4, CX * LY, LANES), F32),
             vmem((4, CX * CY, LANES), F32),
-            vmem((DEVICES, 4, LANES), F32),
-            vmem((DEVICES, 4, LANES), F32),
-            vmem((DEVICES, 4, LANES), F32),
-            vmem((DEVICES, 4, LANES), F32),
+            vmem(wide.shape, F32),
+            vmem(narrow.shape, F32),
+        ] + [vmem((DEVICES, 4, LANES), F32)] * 4 + [
             vmem((3, 2, 4, LX, LANES), F32),
             vmem((3, 2, 4, LY, LANES), F32),
             vmem((3, 2, 4, LX, LANES), F32),
@@ -438,17 +543,35 @@
             vmem((2, 4, CY, LANES), F32),
             vmem((2, 4, CX, LANES), F32),
             vmem((2, 4, CY, LANES), F32),
-            dma((10,)),
             dma((4,)),
+            dma((PARTS, 6)),
+            dma((2,)),
             dma((4,)),
             dma((4, 4)),
             dma((4, 4)),
+            dma((PARTS, 4)),
+            pltpu.SemaphoreType.REGULAR,
         ],
         compiler_params=pltpu.CompilerParams(
-            collective_id=0, has_side_effects=True, vmem_limit_bytes=48 << 20),
+            collective_id=0, has_side_effects=True, vmem_limit_bytes=LIMIT),
         name="schwarz",
-    )(field_now, source, wavenumber_sq, shift_sq, vertical,
-      basis, rows, lanes, unlanes, unrows, twiddle, eigen)
+    )(field_now, source, wavenumber_sq, shift_sq, wide, narrow)
+    return pl.pallas_call(
+        finish,
+        out_shape=jax.ShapeDtypeStruct(field_now.shape, F32),
+        in_specs=[hbm] * 3,
+        out_specs=hbm,
+        scratch_shapes=[
+            vmem((4, LX, LY, LANES), F32),
+            vmem(edges[0], F32),
+            vmem(edges[1], F32),
+            dma((4, 2)),
+            dma((2,)),
+            dma((4, 2)),
+        ],
+        compiler_params=pltpu.CompilerParams(vmem_limit_bytes=LIMIT),
+        name="finish",
+    )(*parts)
 
 
 def solution(mesh):

time: 77.6 us -> 57.6 us (0.74)
  the two profiles are of different devices: /device:TPU:1 before, /device:TPU:24 now
where the time goes in v2:
time: 57.6 us; the launch traced here: 57.5 us
  Pallas kernels  56.8 us (99%)
  between operations  0.66 us (1%)
    pallas_call x1, Pallas kernels, body(): pl.pallas_call(kernel, out_shape=[jax.ShapeDtypeStruct(s, F32) for s in [...  52.5 us
    pallas_call x1, Pallas kernels, body(): pl.pallas_call(finish, out_shape=jax.ShapeDtypeStruct(field_now.shape, F3...  4.29 us

profile of v2, /device:TPU:24, one launch (start us, length us, event | category | flops | bytes accessed | tf_op | source)
XLA Modules:
  0.0 57.5 jit_solution(9269183495204402794)
XLA Ops:
  0.7 52.5 %schwarz.1 = (f32[4,64,32,128]{3,2,1,0:T(8,128)}, f32[2,4,64,128]{3,2,1,0:T(8,128)}, f32[2,4,32,128]{3,2,1,0:T(8,128)}) custom-call(f32[2,64,32,256]{3,2,1,0:T(8,128)} %f_hbm.1, f32[2,64,32,256]{3,2,1,0:T(8,128)} %s_hbm.1, f32[64,32,256]{2,1,0:T(8,128)} %k_hbm.1, f32[1]{0:T(128)S(6)} %copy.7.shift_ref, f32[5,256,256]{2,1,0:T(8,128)} %constant.4.clone.wide_hbm, ...), custom_call_target="tpu_custom_call" | custom-call | tf_op jit(solution)/shard_map/schwarz/pallas_call | solution.py:518
  53.2 4.3 %finish.1 = f32[2,64,32,256]{3,2,1,0:T(8,128)} custom-call(f32[4,64,32,128]{3,2,1,0:T(8,128)} %get-tuple-element.8.parts, f32[2,4,64,128]{3,2,1,0:T(8,128)} %get-tuple-element.9.edge_y_hbm, f32[2,4,32,128]{3,2,1,0:T(8,128)} %get-tuple-element.10.edge_x_hbm), custom_call_target="tpu_custom_call" | custom-call | tf_op jit(solution)/shard_map/finish/pallas_call | solution.py:559

commit v3 on v2

--- a/solution.py
+++ b/solution.py
@@ -108,14 +108,21 @@
     column = [lax.rem(d + j, MEMBERS) for j in range(MEMBERS)]
 
     def everyone(start):
+        order = [(2, 1), (1, 1), (3, 1), (2, 0), (0, 1), (1, 0), (3, 0), (0, 0)]
+        columns = [
+            4 * lax.rem(d // 4 + c, 4) + 2 * lax.rem(d // 2 + e, 2) + lax.rem(d + f, 2)
+            for c, e in order for f in (1, 0)
+        ]
+
         def row(i, carry):
-            tg = lax.rem(g + i, GROUPS)
-            for td in column:
+            i = i + i // 5
+            tg = 4 * lax.rem(g // 4 + 1 + i, 2) + lax.rem(g + 2 + 3 * (i // 2), 4)
+            for td in columns:
                 start(tg, td)
             return carry
 
-        lax.fori_loop(1, GROUPS, row, 0)
-        for td in column[1:]:
+        lax.fori_loop(0, GROUPS - 1, row, 0)
+        for td in columns[:-1]:
             start(g, td)
 
     for ref in (ry, rx, rey, rex):
@@ -201,12 +208,12 @@
         for here, copy, _ in plan:
             pl.when(here)(copy.start)
 
+    sent = []
+
     def finish_sides(plan):
         for here, _, arrived in plan:
-            @pl.when(here)
-            def _(arrived=arrived):
-                arrived.wait_send()
-                arrived.wait_recv()
+            pl.when(here)(arrived.wait_recv)
+            sent.append((here, arrived.wait_send))
 
     def pack(field, e):
         flat = field.reshape(4, PAD_X * PAD_Y, LANES)
@@ -222,6 +229,14 @@
     for copy in loads:
         copy.wait()
     pack(fa, 0)
+    for hc in range(4):
+        for side in range(2):
+            sey[0, side, hc] = sum(
+                sy[0, side, hc, pl.ds(q, CX, stride=4), :] for q in range(4))
+            sex[0, side, hc] = sum(
+                sx[0, side, hc, pl.ds(q, CY, stride=4), :] for q in range(4))
+    sums = sides(4, sey.at[0], sex.at[0], rey.at[0], rex.at[0])
+    start_sides(sums)
     start = beside(0)
     start_sides(start)
 
@@ -257,7 +272,7 @@
     for copy in constants:
         copy.wait()
 
-    finish_sides(start)
+    finish_sides(sums)
     cells = CX * CY
     for hc in range(4):
         value = summed[hc, pl.ds(0, cells, stride=4), :]
@@ -265,12 +280,10 @@
             value = value + summed[hc, pl.ds(q, cells, stride=4), :]
         coarse[hc] = value
         for side in range(2):
-            for q in range(4):
-                at = pl.ds(7 * side, CX, stride=CY)
-                coarse[hc, at, :] = coarse[hc, at, :] + ry[0, side, hc, pl.ds(q, CX, stride=4), :]
-            for q in range(4):
-                at = pl.ds((CX - 1) * CY * side, CY)
-                coarse[hc, at, :] = coarse[hc, at, :] + rx[0, side, hc, pl.ds(q, CY, stride=4), :]
+            at = pl.ds(7 * side, CX, stride=CY)
+            coarse[hc, at, :] = coarse[hc, at, :] + rey[0, side, hc]
+            at = pl.ds((CX - 1) * CY * side, CY)
+            coarse[hc, at, :] = coarse[hc, at, :] + rex[0, side, hc]
 
     mean = jnp.concatenate(
         [jnp.concatenate([coarse[0], coarse[1]], axis=1),
@@ -293,7 +306,8 @@
         everyone(one)
         target[me] = source[me]
         some = pl.ds(0, DEVICES - 1)
-        pltpu.make_async_copy(source.at[some], source.at[some], a2a_sem.at[2 * index]).wait()
+        sent.append((None, pltpu.make_async_copy(
+            source.at[some], source.at[some], a2a_sem.at[2 * index]).wait))
         pltpu.make_async_copy(target.at[some], target.at[some], a2a_sem.at[2 * index + 1]).wait()
 
     pl.semaphore_wait(ready, GROUPS - 1)
@@ -355,9 +369,9 @@
 
     for hc in range(4):
         for side in range(2):
-            sey[side, hc] = coarse[hc, pl.ds(7 * side, CX, stride=CY), :]
-            sex[side, hc] = coarse[hc, pl.ds((CX - 1) * CY * side, CY), :]
-    edges = sides(3, sey, sex, rey, rex)
+            sey[1, side, hc] = coarse[hc, pl.ds(7 * side, CX, stride=CY), :]
+            sex[1, side, hc] = coarse[hc, pl.ds((CX - 1) * CY * side, CY), :]
+    edges = sides(3, sey.at[1], sex.at[1], rey.at[1], rex.at[1])
     start_sides(edges)
 
     def prolong(xi, carry):
@@ -432,14 +446,15 @@
                     weight[h, x] * rx[e, side, hc])
 
     sweep(fa, into(fb))
+    finish_sides(start)
     finish_sides(edges)
     for hc in range(4):
         for side in range(2):
             for q in range(4):
                 at = pl.ds(q, CX, stride=4)
-                ry[0, side, hc, at, :] = ry[0, side, hc, at, :] + rey[side, hc]
+                ry[0, side, hc, at, :] = ry[0, side, hc, at, :] + rey[1, side, hc]
                 at = pl.ds(q, CY, stride=4)
-                rx[0, side, hc, at, :] = rx[0, side, hc, at, :] + rex[side, hc]
+                rx[0, side, hc, at, :] = rx[0, side, hc, at, :] + rex[1, side, hc]
     add_halos(fb, 0)
     pack(fb, 1)
     plan = beside(1)
@@ -465,6 +480,11 @@
     ]
     for copy in last:
         copy.start()
+    for here, wait in sent:
+        if here is None:
+            wait()
+        else:
+            pl.when(here)(wait)
     for i in range(PARTS):
         for copy in stores(i):
             copy.wait()
@@ -539,16 +559,16 @@
             vmem((3, 2, 4, LY, LANES), F32),
             vmem((3, 2, 4, LX, LANES), F32),
             vmem((3, 2, 4, LY, LANES), F32),
-            vmem((2, 4, CX, LANES), F32),
-            vmem((2, 4, CY, LANES), F32),
-            vmem((2, 4, CX, LANES), F32),
-            vmem((2, 4, CY, LANES), F32),
+            vmem((2, 2, 4, CX, LANES), F32),
+            vmem((2, 2, 4, CY, LANES), F32),
+            vmem((2, 2, 4, CX, LANES), F32),
+            vmem((2, 2, 4, CY, LANES), F32),
             dma((4,)),
             dma((PARTS, 6)),
             dma((2,)),
             dma((4,)),
-            dma((4, 4)),
-            dma((4, 4)),
+            dma((5, 4)),
+            dma((5, 4)),
             dma((PARTS, 4)),
             pltpu.SemaphoreType.REGULAR,
         ],

time: 57.6 us -> 54.9 us (0.953)
  Pallas kernels: 56.8 us -> 54.1 us
    pallas_call x1, Pallas kernels: 52.5 us -> 49.8 us  [body(): pl.pallas_call(kernel, out_shape=[jax.ShapeDtypeStruct(s, F32) for s in [...]
where the time goes in v3:
time: 54.9 us; the launch traced here: 54.7 us
  Pallas kernels  54.1 us (99%)
  between operations  0.66 us (1%)
    pallas_call x1, Pallas kernels, body(): pl.pallas_call(kernel, out_shape=[jax.ShapeDtypeStruct(s, F32) for s in [...  49.8 us
    pallas_call x1, Pallas kernels, body(): pl.pallas_call(finish, out_shape=jax.ShapeDtypeStruct(field_now.shape, F3...  4.29 us

profile of v3, /device:TPU:24, one launch (start us, length us, event | category | flops | bytes accessed | tf_op | source)
XLA Modules:
  0.0 54.7 jit_solution(5296396895543428290)
XLA Ops:
  0.7 49.8 %schwarz.1 = (f32[4,64,32,128]{3,2,1,0:T(8,128)}, f32[2,4,64,128]{3,2,1,0:T(8,128)}, f32[2,4,32,128]{3,2,1,0:T(8,128)}) custom-call(f32[2,64,32,256]{3,2,1,0:T(8,128)} %f_hbm.1, f32[2,64,32,256]{3,2,1,0:T(8,128)} %s_hbm.1, f32[64,32,256]{2,1,0:T(8,128)} %k_hbm.1, f32[1]{0:T(128)S(6)} %copy.7.shift_ref, f32[5,256,256]{2,1,0:T(8,128)} %constant.4.clone.wide_hbm, ...), custom_call_target="tpu_custom_call" | custom-call | tf_op jit(solution)/shard_map/schwarz/pallas_call | solution.py:538
  50.4 4.3 %finish.1 = f32[2,64,32,256]{3,2,1,0:T(8,128)} custom-call(f32[4,64,32,128]{3,2,1,0:T(8,128)} %get-tuple-element.8.parts, f32[2,4,64,128]{3,2,1,0:T(8,128)} %get-tuple-element.9.edge_y_hbm, f32[2,4,32,128]{3,2,1,0:T(8,128)} %get-tuple-element.10.edge_x_hbm), custom_call_target="tpu_custom_call" | custom-call | tf_op jit(solution)/shard_map/finish/pallas_call | solution.py:579

commit v4 on v3

--- a/solution.py
+++ b/solution.py
@@ -14,7 +14,6 @@
 LIMIT = 67043328
 RELAX = 0.8
 DAMPING = 0.5
-HIGHEST = lax.Precision.HIGHEST
 MESH = pl.DeviceIdType.MESH
 
 GROUPS, MEMBERS = 8, 16
@@ -59,10 +58,17 @@
 
 
 def dot(a, b, contract):
-    return lax.dot_general(
-        a, b, ((contract[:1], contract[1:]), ((), ())), precision=HIGHEST,
-        preferred_element_type=F32,
-    )
+    def halved(value):
+        high = value.astype(jnp.bfloat16)
+        return high, (value - high.astype(F32)).astype(jnp.bfloat16)
+
+    def product(u, v):
+        return lax.dot_general(
+            u, v, ((contract[:1], contract[1:]), ((), ())), preferred_element_type=F32)
+
+    a_high, a_low = halved(a)
+    b_high, b_low = halved(b)
+    return product(a_high, b_high) + (product(a_high, b_low) + product(a_low, b_high))
 
 
 def stencil(field, x, tile, absorb, lane):
@@ -421,12 +427,12 @@
         return put
 
     def put_out(hc, x, tile, value):
-        res[hc, x, 8 * tile : 8 * tile + 8, :] = value
+        res[hc // 2, x, 8 * tile : 8 * tile + 8, halves[hc % 2]] = value
 
     def stores(i):
         x = pl.ds(i * (LX // PARTS), LX // PARTS)
-        return [pltpu.make_async_copy(res.at[hc, x], out_hbm.at[hc, x], store_sem.at[i, hc])
-                for hc in range(4)]
+        return [pltpu.make_async_copy(res.at[c, x], out_hbm.at[c, x], store_sem.at[i, c])
+                for c in range(2)]
 
     def start_stores(i):
         for copy in stores(i):
@@ -497,33 +503,43 @@
         pltpu.make_async_copy(edge_y_hbm, edge_y, sem_edge.at[0]),
         pltpu.make_async_copy(edge_x_hbm, edge_x, sem_edge.at[1]),
     ]
-    half = LX // 2
-    blocks = [(hc, i) for hc in range(4) for i in range(2)]
-    loads = [
-        pltpu.make_async_copy(
-            parts.at[hc, pl.ds(half * i, half)], field.at[hc, pl.ds(half * i, half)],
-            sem_in.at[hc, i])
-        for hc, i in blocks
-    ]
-    stores = [
-        pltpu.make_async_copy(
-            field.at[hc, pl.ds(half * i, half)],
-            out_hbm.at[hc // 2, pl.ds(half * i, half), :, pl.ds(LANES * (hc % 2), LANES)],
-            sem_out.at[hc, i])
-        for hc, i in blocks
-    ]
+    size = LX // PARTS
+    halves = [slice(LANES * h, LANES * (h + 1)) for h in range(2)]
+    blocks = [(c, i) for c in range(2) for i in range(PARTS)]
+
+    def moves(source, target, sems):
+        return [
+            pltpu.make_async_copy(
+                source.at[c, pl.ds(size * i, size)], target.at[c, pl.ds(size * i, size)],
+                sems.at[c, i])
+            for c, i in blocks
+        ]
+
+    loads = moves(parts, field, sem_in)
+    stores = moves(field, out_hbm, sem_out)
     for copy in edges + loads:
         copy.start()
     for copy in edges:
         copy.wait()
-    flat = field.reshape(4, LX * LY, LANES)
-    for (hc, i), load, store in zip(blocks, loads, stores):
+    for (c, i), load, store in zip(blocks, loads, stores):
         load.wait()
-        for side, row in ((0, 0), (1, LY - 1)):
-            at = pl.ds(half * i * LY + row, half, stride=LY)
-            flat[hc, at, :] = flat[hc, at, :] + edge_y[side, hc, half * i : half * (i + 1), :]
-        x = (LX - 1) * i
-        field[hc, x] = field[hc, x] + edge_x[i, hc]
+
+        def rows(j, carry, c=c, i=i):
+            for u in range(4):
+                x = size * i + 4 * j + u
+                for h in range(2):
+                    for side, row in ((0, slice(0, 1)), (1, slice(LY - 1, LY))):
+                        field[c, x, row, halves[h]] = field[c, x, row, halves[h]] + (
+                            edge_y[side, 2 * c + h, pl.ds(x, 1), :])
+            return carry
+
+        lax.fori_loop(0, size // 4, rows, 0)
+        for side, part in ((0, 0), (1, PARTS - 1)):
+            if i == part:
+                x = (LX - 1) * side
+                for h in range(2):
+                    field[c, x, :, halves[h]] = field[c, x, :, halves[h]] + (
+                        edge_x[side, 2 * c + h])
         store.start()
     for store in stores:
         store.wait()
@@ -537,13 +553,13 @@
     edges = [(2, 4, LX, LANES), (2, 4, LY, LANES)]
     parts = pl.pallas_call(
         kernel,
-        out_shape=[jax.ShapeDtypeStruct(s, F32) for s in [(4, LX, LY, LANES)] + edges],
+        out_shape=[jax.ShapeDtypeStruct(s, F32) for s in [field_now.shape] + edges],
         in_specs=[hbm] * 3 + [pl.BlockSpec(memory_space=pltpu.SMEM)] + [hbm] * 2,
         out_specs=[hbm] * 3,
         scratch_shapes=[
             vmem((4, PAD_X, PAD_Y, LANES), F32),
             vmem((4, PAD_X, PAD_Y, LANES), F32),
-            vmem((4, LX, LY, LANES), F32),
+            vmem(field_now.shape, F32),
             vmem(edges[0], F32),
             vmem(edges[1], F32),
             vmem((4, LX, LY, LANES), F32),
@@ -569,7 +585,7 @@
             dma((4,)),
             dma((5, 4)),
             dma((5, 4)),
-            dma((PARTS, 4)),
+            dma((PARTS, 2)),
             pltpu.SemaphoreType.REGULAR,
         ],
         compiler_params=pltpu.CompilerParams(
@@ -582,12 +598,12 @@
         in_specs=[hbm] * 3,
         out_specs=hbm,
         scratch_shapes=[
-            vmem((4, LX, LY, LANES), F32),
+            vmem(field_now.shape, F32),
             vmem(edges[0], F32),
             vmem(edges[1], F32),
-            dma((4, 2)),
+            dma((2, PARTS)),
             dma((2,)),
-            dma((4, 2)),
+            dma((2, PARTS)),
         ],
         compiler_params=pltpu.CompilerParams(vmem_limit_bytes=LIMIT),
         name="finish",

time: 54.9 us -> 53.5 us (0.974)
  Pallas kernels: 54.1 us -> 52.7 us
    pallas_call x1, Pallas kernels: 49.8 us -> 48.4 us  [body(): pl.pallas_call(kernel, out_shape=[jax.ShapeDtypeStruct(s, F32) for s in [...]
where the time goes in v4:
time: 53.5 us; the launch traced here: 53.4 us
  Pallas kernels  52.7 us (99%)
  between operations  0.66 us (1%)
    pallas_call x1, Pallas kernels, body(): pl.pallas_call(kernel, out_shape=[jax.ShapeDtypeStruct(s, F32) for s in [...  48.4 us
    pallas_call x1, Pallas kernels, body(): pl.pallas_call(finish, out_shape=jax.ShapeDtypeStruct(field_now.shape, F3...  4.3 us

profile of v4, /device:TPU:24, one launch (start us, length us, event | category | flops | bytes accessed | tf_op | source)
XLA Modules:
  0.0 53.4 jit_solution(11868506334222582013)
XLA Ops:
  0.7 48.4 %schwarz.1 = (f32[2,64,32,256]{3,2,1,0:T(8,128)}, f32[2,4,64,128]{3,2,1,0:T(8,128)}, f32[2,4,32,128]{3,2,1,0:T(8,128)}) custom-call(f32[2,64,32,256]{3,2,1,0:T(8,128)} %f_hbm.1, f32[2,64,32,256]{3,2,1,0:T(8,128)} %s_hbm.1, f32[64,32,256]{2,1,0:T(8,128)} %k_hbm.1, f32[1]{0:T(128)S(6)} %copy.7.shift_ref, f32[5,256,256]{2,1,0:T(8,128)} %constant.4.clone.wide_hbm, ...), custom_call_target="tpu_custom_call" | custom-call | tf_op jit(solution)/shard_map/schwarz/pallas_call | solution.py:554
  49.1 4.3 %finish.1 = f32[2,64,32,256]{3,2,1,0:T(8,128)} custom-call(f32[2,64,32,256]{3,2,1,0:T(8,128)} %get-tuple-element.8.parts, f32[2,4,64,128]{3,2,1,0:T(8,128)} %get-tuple-element.9.edge_y_hbm, f32[2,4,32,128]{3,2,1,0:T(8,128)} %get-tuple-element.10.edge_x_hbm), custom_call_target="tpu_custom_call" | custom-call | tf_op jit(solution)/shard_map/finish/pallas_call | solution.py:595

commit v5 on v4

--- a/solution.py
+++ b/solution.py
@@ -243,8 +243,6 @@
                 sx[0, side, hc, pl.ds(q, CY, stride=4), :] for q in range(4))
     sums = sides(4, sey.at[0], sex.at[0], rey.at[0], rex.at[0])
     start_sides(sums)
-    start = beside(0)
-    start_sides(start)
 
     lane = lax.broadcasted_iota(jnp.int32, (8, LANES), 1)
     sub = lax.broadcasted_iota(jnp.int32, (8, LANES), 0)
@@ -318,6 +316,8 @@
 
     pl.semaphore_wait(ready, GROUPS - 1)
     to_all(send1, recv1, 0)
+    start = beside(0)
+    start_sides(start)
 
     recv1_flat = recv1.reshape(4 * DEVICES, LANES)
     part = [recv1_flat[pl.ds(q, DEVICES, stride=4), :] for q in range(4)]

time: 53.5 us -> 52.9 us (0.989)
  Pallas kernels: 52.7 us -> 52.1 us
    pallas_call x1, Pallas kernels: 48.4 us -> 47.8 us  [body(): pl.pallas_call(kernel, out_shape=[jax.ShapeDtypeStruct(s, F32) for s in [...]
where the time goes in v5:
time: 52.9 us; the launch traced here: 52.7 us
  Pallas kernels  52.1 us (98%)
  between operations  0.66 us (1%)
    pallas_call x1, Pallas kernels, body(): pl.pallas_call(kernel, out_shape=[jax.ShapeDtypeStruct(s, F32) for s in [...  47.8 us
    pallas_call x1, Pallas kernels, body(): pl.pallas_call(finish, out_shape=jax.ShapeDtypeStruct(field_now.shape, F3...  4.3 us

profile of v5, /device:TPU:24, one launch (start us, length us, event | category | flops | bytes accessed | tf_op | source)
XLA Modules:
  0.0 52.7 jit_solution(3008573493976341444)
XLA Ops:
  0.7 47.8 %schwarz.1 = (f32[2,64,32,256]{3,2,1,0:T(8,128)}, f32[2,4,64,128]{3,2,1,0:T(8,128)}, f32[2,4,32,128]{3,2,1,0:T(8,128)}) custom-call(f32[2,64,32,256]{3,2,1,0:T(8,128)} %f_hbm.1, f32[2,64,32,256]{3,2,1,0:T(8,128)} %s_hbm.1, f32[64,32,256]{2,1,0:T(8,128)} %k_hbm.1, f32[1]{0:T(128)S(6)} %copy.7.shift_ref, f32[5,256,256]{2,1,0:T(8,128)} %constant.4.clone.wide_hbm, ...), custom_call_target="tpu_custom_call" | custom-call | tf_op jit(solution)/shard_map/schwarz/pallas_call | solution.py:554
  48.4 4.3 %finish.1 = f32[2,64,32,256]{3,2,1,0:T(8,128)} custom-call(f32[2,64,32,256]{3,2,1,0:T(8,128)} %get-tuple-element.8.parts, f32[2,4,64,128]{3,2,1,0:T(8,128)} %get-tuple-element.9.edge_y_hbm, f32[2,4,32,128]{3,2,1,0:T(8,128)} %get-tuple-element.10.edge_x_hbm), custom_call_target="tpu_custom_call" | custom-call | tf_op jit(solution)/shard_map/finish/pallas_call | solution.py:595

commit v6 on v5

--- a/solution.py
+++ b/solution.py
@@ -20,7 +20,7 @@
 DEVICES = GROUPS * MEMBERS
 LX, LY, NZ = 64, 32, 256
 CX, CY = LX // 4, LY // 4
-PARTS = 4
+PARTS = 8
 PAD_X, PAD_Y = LX + 2, LY + 16
 LANES = 128
 TILES = LY // 8

time: 52.9 us -> 53.4 us (level)
  no operation moved by 1% of the time
where the time goes in v6:
time: 53.4 us; the launch traced here: 53.3 us
  Pallas kernels  52.6 us (99%)
  between operations  0.66 us (1%)
    pallas_call x1, Pallas kernels, body(): pl.pallas_call(kernel, out_shape=[jax.ShapeDtypeStruct(s, F32) for s in [...  48.1 us
    pallas_call x1, Pallas kernels, body(): pl.pallas_call(finish, out_shape=jax.ShapeDtypeStruct(field_now.shape, F3...  4.48 us

profile of v6, /device:TPU:24, one launch (start us, length us, event | category | flops | bytes accessed | tf_op | source)
XLA Modules:
  0.0 53.3 jit_solution(16535966569525910119)
XLA Ops:
  0.7 48.1 %schwarz.1 = (f32[2,64,32,256]{3,2,1,0:T(8,128)}, f32[2,4,64,128]{3,2,1,0:T(8,128)}, f32[2,4,32,128]{3,2,1,0:T(8,128)}) custom-call(f32[2,64,32,256]{3,2,1,0:T(8,128)} %f_hbm.1, f32[2,64,32,256]{3,2,1,0:T(8,128)} %s_hbm.1, f32[64,32,256]{2,1,0:T(8,128)} %k_hbm.1, f32[1]{0:T(128)S(6)} %copy.7.shift_ref, f32[5,256,256]{2,1,0:T(8,128)} %constant.4.clone.wide_hbm, ...), custom_call_target="tpu_custom_call" | custom-call | tf_op jit(solution)/shard_map/schwarz/pallas_call | solution.py:554
  48.8 4.5 %finish.1 = f32[2,64,32,256]{3,2,1,0:T(8,128)} custom-call(f32[2,64,32,256]{3,2,1,0:T(8,128)} %get-tuple-element.8.parts, f32[2,4,64,128]{3,2,1,0:T(8,128)} %get-tuple-element.9.edge_y_hbm, f32[2,4,32,128]{3,2,1,0:T(8,128)} %get-tuple-element.10.edge_x_hbm), custom_call_target="tpu_custom_call" | custom-call | tf_op jit(solution)/shard_map/finish/pallas_call | solution.py:595
